TPU v7x, 512 devices: a whole 4x4x16 slice. The times are simulated.
512 devices in a mesh: row: 32 (over z_hi, y, core), col: 16 (over z_lo, x).
Axes of the slice: x: 4, y: 4, z: 16 (z_hi: 4, z_lo: 4; z = z_hi * 4 + z_lo), core: 2. Of those that a mesh axis runs over, the one named last changes fastest.
Arguments:
- hidden: bfloat16 [256, 2048], P('row', 'col'), may hold values from -60 to 60
- queries: bfloat16 [256, 4096], P('row'), may hold values from -6 to 6
- new_kv: bfloat16 [256, 2, 2048], P('row'), may hold values from -12 to 12
- prompt_kv: bfloat16 [32, 2, 1024, 2048], P('row', None, 'col'), may hold values from -180 to 180
- suffix_kv: bfloat16 [256, 2, 128, 2048], P('row', None, 'col'), may hold values from -12 to 12
- lengths: int32 [256], P('row'), may hold values from 1 to 128, as said below
- w_out: bfloat16 [4096, 2048], P(None, 'col'), may hold values from -0.375 to 0.375
- moe_gain: bfloat16 [2048], P('col'), may hold values from 0.099609375 to 1.8984375
- w_router: bfloat16 [2048, 8], P('col'), may hold values from -0.5 to 0.5
- expert_weights: bfloat16 [8, 5632, 3, 2048], P(None, 'row', None, 'col'), may hold values from -0.25 to 0.25
- old_lines: int32 [8, 5632], replicated, may hold values from 0 to 5631, as said below
- new_lines: int32 [8, 5632], replicated, may hold values from 0 to 5631, as said below
- routes: int32 [256, 2], replicated, may hold values from 0 to 7, all different within a row
Outputs:
- layer_out: float32 [256, 2048], P('row', 'col')
- moved_weights: bfloat16 [8, 5632, 3, 2048], P(None, 'row', None, 'col')
Inputs may be any that keep to these rules, and one draw needn't show every extreme that they name: `lengths`: some sequence has all 128 slots filled. `old_lines`: each row is a permutation of the hidden units of one expert; stored lines [j * 176, (j + 1) * 176) lie on row index j. `new_lines`: each row is a permutation of the hidden units of one expert. Counting all experts together, exactly 44 of the lines that one row index holds under old_lines are held by each row index under new_lines. `routes`: the two experts of a token differ.
All inputs are finite; a program needn't handle non-finite values.
Results may differ from a plain program's by a relative error of at most 0.04.
Values may be sent and summed in bfloat16 or wider, within the bound.
A program may use at most 64 MiB of HBM per device.

v0:
```python
import jax
import jax.numpy as jnp
from jax import lax
from jax.sharding import PartitionSpec as P

D = 2048
KVH = 16
HD = 128
REP = 2


norm_eps = 1e-06
neg_big = -1e30


def joined(part, axis, combine):
    gathered = jax.tree.map(lambda a: lax.all_gather(a, axis), part)

    def take(source):
        return jax.tree.map(lambda a: lax.dynamic_index_in_dim(a, source, 0, False), gathered)

    return lax.fori_loop(
        1, lax.axis_size(axis), lambda source, state: combine(state, take(source)), take(0)
    )


def merge_partial(earlier, following):
    highest_a, totals_a, mixture_a = earlier
    highest_b, totals_b, mixture_b = following
    highest = jnp.maximum(highest_a, highest_b)
    factor_a = jnp.exp(highest_a - highest)
    factor_b = jnp.exp(highest_b - highest)
    return (
        highest,
        totals_a * factor_a + totals_b * factor_b,
        mixture_a * factor_a[..., None] + mixture_b * factor_b[..., None],
    )


def attend(queries, new_kv, prompt_kv, suffix_kv, lengths):
    seq_count = queries.shape[0]
    prompt_rows = prompt_kv.shape[2]
    suffix_rows = suffix_kv.shape[2]
    col_index = lax.axis_index("col")
    query_heads = queries.reshape(seq_count, KVH, REP, HD)
    prompt_keys = prompt_kv[0, 0].reshape(prompt_rows, KVH, HD)
    prompt_values = prompt_kv[0, 1].reshape(prompt_rows, KVH, HD)
    suffix_keys = suffix_kv[:, 0].reshape(seq_count, suffix_rows, KVH, HD)
    suffix_values = suffix_kv[:, 1].reshape(seq_count, suffix_rows, KVH, HD)
    own_keys = new_kv[:, 0].reshape(seq_count, KVH, HD)
    own_values = new_kv[:, 1].reshape(seq_count, KVH, HD)
    score_scale = HD ** (-0.5)
    prompt_scores = (
        jnp.einsum("skgd,pkd->skgp", query_heads, prompt_keys, preferred_element_type=jnp.float32)
        * score_scale
    )
    suffix_scores = (
        jnp.einsum("skgd,spkd->skgp", query_heads, suffix_keys, preferred_element_type=jnp.float32)
        * score_scale
    )
    own_scores = (
        jnp.einsum("skgd,skd->skg", query_heads, own_keys, preferred_element_type=jnp.float32)
        * score_scale
    )
    positions = col_index * suffix_rows + jnp.arange(suffix_rows, dtype=jnp.int32)
    live_slots = (positions[None, :] < lengths[:, None])[:, None, None, :]
    holder = col_index == 0
    suffix_scores = jnp.where(live_slots, suffix_scores, neg_big)
    own_scores = jnp.where(holder, own_scores, neg_big)
    highest = jnp.maximum(
        jnp.maximum(jnp.max(prompt_scores, axis=-1), jnp.max(suffix_scores, axis=-1)), own_scores
    )
    prompt_weights = jnp.exp(prompt_scores - highest[..., None])
    suffix_weights = jnp.where(live_slots, jnp.exp(suffix_scores - highest[..., None]), 0.0)
    own_weights = jnp.where(holder, jnp.exp(own_scores - highest), 0.0)
    totals = jnp.sum(prompt_weights, axis=-1) + jnp.sum(suffix_weights, axis=-1) + own_weights
    mixture = jnp.einsum(
        "skgp,pkd->skgd",
        prompt_weights.astype(jnp.bfloat16),
        prompt_values,
        preferred_element_type=jnp.float32,
    )
    mixture = mixture + jnp.einsum(
        "skgp,spkd->skgd",
        suffix_weights.astype(jnp.bfloat16),
        suffix_values,
        preferred_element_type=jnp.float32,
    )
    own_rounded = lax.optimization_barrier(own_weights.astype(jnp.bfloat16)).astype(jnp.float32)
    mixture = mixture + own_rounded[..., None] * own_values.astype(jnp.float32)[:, :, None, :]
    highest, totals, mixture = joined((highest, totals, mixture), "col", merge_partial)
    return (mixture / totals[..., None]).astype(jnp.bfloat16).reshape(seq_count, -1)


def inverse_rows(table):
    expert_count, full_width = table.shape
    row_ids = jnp.broadcast_to(jnp.arange(expert_count, dtype=jnp.int32)[:, None], table.shape)
    slot_ids = jnp.broadcast_to(jnp.arange(full_width, dtype=jnp.int32)[None, :], table.shape)
    return jnp.zeros_like(table).at[row_ids, table].set(slot_ids)


def migrate(expert_weights, old_lines, new_lines):
    row_count = lax.axis_size("row")
    row_index = lax.axis_index("row")
    expert_count, line_count, three_parts, width_col = expert_weights.shape
    full_width = old_lines.shape[1]
    unit_count = expert_count * line_count
    per_peer = unit_count // row_count
    inverse_old = inverse_rows(old_lines)
    inverse_new = inverse_rows(new_lines)
    held_ids = lax.dynamic_slice_in_dim(old_lines, row_index * line_count, line_count, 1)
    target_slots = jnp.take_along_axis(inverse_new, held_ids, axis=1)
    expert_ids = jnp.arange(expert_count, dtype=jnp.int32)[:, None]
    sort_keys = (
        target_slots // line_count * (expert_count * full_width)
        + expert_ids * full_width
        + target_slots
    )
    sort_order = jnp.argsort(sort_keys.reshape(-1))
    flat_units = expert_weights.reshape(unit_count, three_parts, width_col)
    outgoing = flat_units[sort_order].reshape(row_count, per_peer, three_parts, width_col)
    arrived = lax.all_to_all(outgoing, "row", split_axis=0, concat_axis=0, tiled=True).reshape(
        unit_count, three_parts, width_col
    )
    wanted_ids = lax.dynamic_slice_in_dim(new_lines, row_index * line_count, line_count, 1)
    anchor_rows = (jnp.take_along_axis(inverse_old, wanted_ids, axis=1) // line_count).reshape(-1)
    anchor_hits = (anchor_rows[:, None] == jnp.arange(row_count, dtype=jnp.int32)[None, :]).astype(
        jnp.int32
    )
    rank_within = jnp.sum(jnp.cumsum(anchor_hits, axis=0) * anchor_hits, axis=1) - 1
    arrived_slot = anchor_rows * per_peer + rank_within
    return arrived[arrived_slot].reshape(expert_count, line_count, three_parts, width_col)


def activate(summed, router_sum, square_sum, chosen):
    inverse_rms = lax.rsqrt(square_sum / D + norm_eps)
    logits = router_sum * inverse_rms[:, None]
    expert_hits = chosen[:, :, None] == jnp.arange(logits.shape[1], dtype=jnp.int32)[None, None, :]
    selected = jnp.sum(jnp.where(expert_hits, logits[:, None, :], 0.0), axis=-1)
    gates = jax.nn.softmax(selected, axis=-1)
    gate_part = summed[:, :, 0] * inverse_rms[:, None, None]
    up_part = summed[:, :, 1] * inverse_rms[:, None, None]
    activated = (jax.nn.silu(gate_part) * up_part).astype(jnp.bfloat16)
    return (gates, activated)


def local(
    hidden,
    queries,
    new_kv,
    prompt_kv,
    suffix_kv,
    lengths,
    w_out,
    moe_gain,
    w_router,
    expert_weights,
    old_lines,
    new_lines,
    routes,
):
    moved_weights = migrate(expert_weights, old_lines, new_lines)
    attended = attend(queries, new_kv, prompt_kv, suffix_kv, lengths)
    projected = jnp.dot(attended, w_out, preferred_element_type=jnp.float32)
    h_mid = (hidden.astype(jnp.float32) + projected).astype(jnp.bfloat16)
    h_float = h_mid.astype(jnp.float32)
    scaled = (h_float * moe_gain.astype(jnp.float32)[None, :]).astype(jnp.bfloat16)
    squares = jnp.sum(h_float * h_float, axis=1)
    every_token, every_square = (
        lax.all_gather(scaled, "row", axis=0, tiled=True),
        lax.all_gather(squares.astype(jnp.bfloat16), "row", axis=0, tiled=True).astype(
            squares.dtype
        ),
    )
    token_total = every_token.shape[0]
    router_part = jnp.dot(every_token, w_router, preferred_element_type=jnp.float32)
    gate_up = jnp.einsum(
        "td,efjd->etjf",
        every_token,
        expert_weights[:, :, :2, :],
        preferred_element_type=jnp.float32,
    )
    picked = gate_up[routes, jnp.arange(token_total, dtype=jnp.int32)[:, None]]
    summed, router_sum, square_sum = lax.psum((picked, router_part, every_square), "col")
    gates, activated = activate(summed, router_sum, square_sum, routes)
    down_lines = expert_weights[:, :, 2, :]
    top_count = routes.shape[1]
    every_expert = jnp.einsum(
        "tkf,efd->etkd", activated, down_lines, preferred_element_type=jnp.float32
    )
    chosen_out = every_expert[
        routes,
        jnp.arange(hidden.shape[0] * lax.axis_size("row"), dtype=jnp.int32)[:, None],
        jnp.arange(top_count, dtype=jnp.int32)[None, :],
    ]
    mixed = lax.psum_scatter(
        jnp.sum(chosen_out * gates[:, :, None], axis=1), "row", scatter_dimension=0, tiled=True
    )
    layer_out = h_float + mixed
    return (layer_out, moved_weights)


def solution(mesh):
    return jax.shard_map(
        local,
        mesh=mesh,
        in_specs=(
            P("row", "col"),
            P("row", None),
            P("row", None, None),
            P("row", None, "col", None),
            P("row", None, "col", None),
            P("row"),
            P(None, "col"),
            P("col"),
            P("col", None),
            P(None, "row", None, "col"),
            P(),
            P(),
            P(),
        ),
        out_specs=(P("row", "col"), P(None, "row", None, "col")),
        check_vma=False,
    )
```

profile of v0, /device:TPU:1, one launch (start us, length us, event | category | flops | bytes accessed | tf_op | source)
XLA Modules:
  0.0 1099.8 jit_solution(18043587728457277030)
XLA Ops:
  7.3 1.2 fusion.38
  8.6 1.1 slice_bitcast_fusion.2
  12.7 6.7 copy.177
  21.3 165.0 %scatter_custom_fusion = s32[45056]{0:T(1024)S(1)} fusion(s32[45056]{0:T(1024)} %reshape.244, s32[45056]{0:T(1024)} %reshape.246, s32[]{:T(128)} %constant.115.clone.1), kind=kCustom, calls=%fused_computation.72 | custom fusion | bytes 180736
  187.2 8.6 gather_fusion.4
  196.1 5.0 sort.17
  201.1 5.2 gather_fusion.2
  206.3 2.6 copy.179
  208.9 19.4 %all-to-all-start = ((bf16[32,44,3,128]{3,1,2,0:T(8,128)(2,1)}), bf16[32,44,3,128]{3,1,2,0:T(8,128)(2,1)}, u32[]{:S(2)}, u32[]{:S(2)}) async-start(bf16[32,44,3,128]{3,1,2,0:T(8,128)(2,1)} %copy.179), calls=%async_computation | async-start | bytes 2359296 | tf_op jit(solution)/shard_map/all_to_all | solution.py:122
  228.4 165.3 %scatter_custom_fusion.1 = s32[45056]{0:T(1024)S(1)} fusion(s32[45056]{0:T(1024)S(1)} %reshape.250, s32[45056]{0:T(1024)} %reshape.246, s32[]{:T(128)} %constant.115.clone.1), kind=kCustom, calls=%fused_computation.70 | custom fusion | bytes 180736
  393.9 8.6 gather_fusion.5
  403.6 34.4 %all-gather = f32[128,16,2]{1,2,0:T(2,128)S(1)} all-gather(f32[8,16,2]{1,2,0:T(2,128)S(1)} %copy.156), channel_id=2, replica_groups=mesh['row'=32,'col'=16] {'col'}, dimensions={0}, use_global_device_ids=true | all-gather | bytes 17408 | tf_op jit(solution)/shard_map/all_gather | solution.py:17
  438.9 30.4 %all-gather.1 = f32[128,16,2]{1,2,0:T(2,128)S(1)} all-gather(f32[8,16,2]{1,2,0:T(2,128)S(1)} %copy.161), channel_id=3, replica_groups=mesh['row'=32,'col'=16] {'col'}, dimensions={0}, use_global_device_ids=true | all-gather | bytes 17408 | tf_op jit(solution)/shard_map/all_gather | solution.py:17
  470.6 9.1 reduce-window.6
  482.6 30.4 %while.19 = (s32[]{:T(128)}, f32[8,16,2]{1,2,0:T(2,128)S(1)}, f32[8,16,2]{1,2,0:T(2,128)S(1)}, f32[8,16,2,128]{3,2,1,0:T(2,128)S(1)}, f32[16,8,16,2]{2,3,1,0:T(2...) while((s32[]{:T(128)}, f32[8,16,2]{1,2,0:T(2,128)S(1)}, ...), condition=%wide.region_5.6_spmd, body=%wide.region_4.5_spmd.sunk | while | flops 99845 | bytes 669847 | solution.py:22
  513.8 68.4 %all_gather.30 = bf16[256,128]{1,0:T(8,128)(2,1)S(1)} all-gather(bf16[8,128]{1,0:T(8,128)(2,1)S(1)} %get-tuple-element.267), channel_id=1, replica_groups=mesh['row'=32,'col'=16] {'row'}, dimensions={0}, use_global_device_ids=true | all-gather | bytes 67584 | tf_op jit(solution)/shard_map/all_gather | solution.py:170
  582.2 2.1 convolution_bitcast_fusion
  584.3 6.9 copy.170
  591.2 5.1 gather_fusion
  596.3 1.3 copy.171
  598.0 83.8 %all-reduce = bf16[256]{0:T(256)(128)(2,1)S(1)} all-reduce(bf16[256]{0:T(256)(128)(2,1)S(1)} %dynamic-update-slice), channel_id=1, replica_groups=mesh['row'=32,'col'=16] {'row'}, use_global_device_ids=true, to_apply=%add | all-reduce | flops 256 | bytes 1024
  681.9 33.7 %all-reduce.2 = (f32[256]{0:T(256)S(1)}, f32[256,8]{0,1:T(8,128)S(1)}) all-reduce(bf16[256]{0:T(256)(128)(2,1)S(1)} %all-reduce, f32[256,8]{0,1:T(8,128)S(1)} %fusion.62), channel_id=1, replica_groups=mesh['row'=32,'col'=16] {'col'}, use_global_device_ids=true, to_apply=%region_8.9 | all-reduce | flops 2304 | bytes 17920 | tf_op jit(solution)/shard_map/psum | solution.py:184
  715.9 36.3 %all-reduce.6.cloned.1.call-done = f32[256,2,2,176]{0,3,2,1:T(8,128)} async-done(((f32[256,2,2,176]{0,3,2,1:T(8,128)}), f32[256,2,2,176]{0,3,2,1:T(8,128)}) %all-reduce.6.cloned.1.call-update) | async-done | bytes 720912 | tf_op jit(solution)/shard_map/psum | solution.py:184
  752.2 1.6 convolution_bitcast_fusion.1
  753.8 1.6 copy.174
  755.4 2.9 gather_fusion.1
  758.3 1.0 multiply_reduce_fusion.2
  760.7 1.8 copy.198
  762.6 5.2 gather_fusion.3
  767.7 2.5 copy.185
  770.2 321.7 %all-reduce.8.cloned.1.call-done = f32[256,128]{1,0:T(8,128)} async-done(((f32[256,128]{1,0:T(8,128)}), f32[256,128]{1,0:T(8,128)}) %all-reduce.8.cloned.1.call-update) | async-done | bytes 131088
  1092.0 1.3 dynamic-slice_add_fusion
  (210 shorter events, 43.7 us)
Async XLA Ops:
  7.2 506.3 %copy-start = (bf16[4096,128]{1,0:T(8,128)(2,1)S(1)}, bf16[4096,128]{1,0:T(8,128)(2,1)}, u32[]{:S(2)}) copy-start(bf16[4096,128]{1,0:T(8,128)(2,1)} %param.23) | copy-start | bytes 3145732
  7.2 2.6 copy-start.8
  7.2 3.0 copy-start.16
  7.2 3.1 copy-start.18
  7.2 474.4 %all-gather.5.cloned.1.call-start = ((), (), s32[]{:S(2)}) async-start(), calls=%async_computation.2 | async-start | bytes 2228224 | tf_op jit(solution)/shard_map/all_gather | solution.py:17
  9.7 1.3 copy-start.7
  10.3 1.3 copy-start.10
  10.9 1.7 copy-start.5
  11.2 1.3 copy-start.1
  12.6 6.8 copy-start.3
  12.6 6.8 copy-start.4
  12.7 6.9 copy-start.17
  12.7 7.0 copy-start.14
  208.9 551.8 %all-to-all-start = ((bf16[32,44,3,128]{3,1,2,0:T(8,128)(2,1)}), bf16[32,44,3,128]{3,1,2,0:T(8,128)(2,1)}, u32[]{:S(2)}, u32[]{:S(2)}) async-start(bf16[32,44,3,128]{3,1,2,0:T(8,128)(2,1)} %copy.179), calls=%async_computation | async-start | bytes 2359296 | tf_op jit(solution)/shard_map/all_to_all | solution.py:122
  228.3 523.8 %all-reduce.6.cloned.1.call-start = ((), (), s32[]{:S(2)}) async-start(), calls=%async_computation.1 | async-start | bytes 1441792 | tf_op jit(solution)/shard_map/psum | solution.py:184
  393.9 9.7 copy-start.19
  393.9 44.1 %copy-start.6 = (f32[8,16,2]{0,2,1:T(2,128)S(1)}, f32[8,16,2]{0,2,1:T(2,128)}, u32[]{:S(2)}) copy-start(f32[8,16,2]{0,2,1:T(2,128)} %copy-done.5) | copy-start | bytes 3076
  393.9 44.4 %copy-start.11 = (pred[8,8]{1,0:T(8,128)(4,1)S(1)}, pred[8,8]{1,0:T(8,128)(4,1)}, u32[]{:S(2)}) copy-start(pred[8,8]{1,0:T(8,128)(4,1)} %copy-done.10) | copy-start | bytes 196
  393.9 75.4 %copy-start.9 = (s32[256,2]{0,1:T(2,128)S(1)}, s32[256,2]{0,1:T(2,128)}, u32[]{:S(2)}) copy-start(s32[256,2]{0,1:T(2,128)} %param.29) | copy-start | bytes 6148
  438.0 42.1 %copy-start.15 = (u32[512]{0:T(512)S(1)}, u32[512]{0:T(512)}, u32[]{:S(2)}) copy-start(u32[512]{0:T(512)} %constant.216) | copy-start | bytes 6148
  482.6 30.8 %copy-start.12 = (bf16[8,128]{1,0:T(8,128)(2,1)S(1)}, bf16[8,128]{1,0:T(8,128)(2,1)}, u32[]{:S(2)}) copy-start(bf16[8,128]{1,0:T(8,128)(2,1)} %param.17) | copy-start | bytes 6148
  513.0 69.2 %copy-start.2 = (bf16[8,176,3,128]{3,1,2,0:T(8,128)(2,1)S(1)}, bf16[8,176,3,128]{3,1,2,0:T(8,128)(2,1)}, u32[]{:S(2)}) copy-start(bf16[8,176,3,128]{3,1,2,0:T(8,128)(2,1)} %param.26) | copy-start | bytes 3244036
  596.3 85.5 %copy-start.13 = (bf16[128,8]{0,1:T(8,128)(2,1)S(1)}, bf16[128,8]{0,1:T(8,128)(2,1)}, u32[]{:S(2)}) copy-start(bf16[128,8]{0,1:T(8,128)(2,1)} %param.25) | copy-start | bytes 6148
  597.7 494.3 %all-reduce.8.cloned.1.call-start = ((), (), s32[]{:S(2)}) async-start(), calls=%async_computation.3 | async-start | bytes 262144
Sparse Core Ops, SparseCore 0:
  12.7 75.4 all-gather.4
  597.8 154.3 all-reduce.5
  759.4 332.4 all-reduce.7
where the time goes:
time: 1100 us
  local copies, waits for them, and re-layouts  415 us (38%)
  waiting for transfers between devices  358 us (33%)
  blocking collectives  251 us (23%)
  other arithmetic  33.2 us (3%)
  starting transfers between devices  19.6 us (2%)
  between operations  15.8 us (1%)
    unnamed x52, local copies, waits for them, and re-layouts  336 us
    unnamed x4, waiting for transfers between devices  322 us
    unnamed x1, blocking collectives  83.8 us
    all_gather x1, blocking collectives, local(): lax.all_gather(scaled, 'row', axis=0, tiled=True)  68.4 us
    all_gather x2, blocking collectives, joined(): gathered = jax.tree.map(lambda a: lax.all_gather(a, axis), part)  64.9 us
    psum x1, waiting for transfers between devices, local(): lax.psum((picked, router_part, every_square), 'col')  36.3 us
    psum x1, blocking collectives, local(): lax.psum((picked, router_part, every_square), 'col')  33.7 us
  transfers between devices with their start and end apart: 4, of which 2 were waited for; matrix products, arithmetic and copies ran while one was open for 41% of the time, Pallas kernels for 0%

commit v1 on v0

v1 whole, which is shorter than its diff:
```python
import functools

import jax
import jax.numpy as jnp
from jax import lax
from jax.experimental import pallas as pl
from jax.experimental.pallas import tpu as pltpu
from jax.sharding import PartitionSpec as P

HD = 128
norm_eps = 1e-06
neg_big = -1e30
f32 = jnp.float32
bf16 = jnp.bfloat16
MESH = pl.DeviceIdType.MESH


def rounded_up(value, step):
    return (value + step - 1) // step * step


def dot_nt(a, b):
    return lax.dot_general(a, b, (((1,), (1,)), ((), ())), preferred_element_type=f32)


def step_kernel(
    row_count,
    col_count,
    lengths_ref,
    hidden_ref,
    queries_ref,
    new_kv_ref,
    prompt_ref,
    suffix_ref,
    w_out_ref,
    gain_ref,
    router_ref,
    lines_ref,
    send_slot_ref,
    take_slot_ref,
    routes_ref,
    layer_ref,
    moved_ref,
    part_out,
    part_in,
    heads_in,
    token_out,
    token_in,
    wide,
    summed_out,
    summed_in,
    act_out,
    act_in,
    down,
    mixed_out,
    mixed_in,
    move_out,
    move_in,
    send_sems,
    recv_sems,
):
    row = lax.axis_index("row")
    col = lax.axis_index("col")
    seqs = hidden_ref.shape[0]
    experts, _, line_count, width = lines_ref.shape
    prompt_rows = prompt_ref.shape[2]
    suffix_rows = suffix_ref.shape[2]
    tokens = seqs * row_count
    share = tokens // col_count
    score_scale = HD ** (-0.5)

    barrier = pltpu.get_barrier_semaphore()

    def greet(axis, me, count):
        def body(k, carry):
            pl.semaphore_signal(
                barrier, inc=1, device_id={axis: lax.rem(me + k, count)}, device_id_type=MESH
            )
            return carry

        lax.fori_loop(1, count, body, 0)

    greet("col", col, col_count)
    greet("row", row, row_count)

    def send(axis, me, count, lane, source, target):
        def body(k, carry):
            peer = lax.rem(me + k, count)
            pltpu.make_async_remote_copy(
                src_ref=source(peer),
                dst_ref=target(k),
                send_sem=send_sems.at[lane],
                recv_sem=recv_sems.at[lane],
                device_id={axis: peer},
                device_id_type=MESH,
            ).start()
            return carry

        lax.fori_loop(1, count, body, 0)

    def wait(count, lane, buffer, sems):
        whole = buffer.at[pl.ds(1, count - 1)]
        pltpu.make_async_copy(whole, whole, sems.at[lane]).wait()

    rows = 2 * seqs
    keys = prompt_rows + seqs * suffix_rows
    row_seq = lax.broadcasted_iota(jnp.int32, (rows, keys), 0) % seqs
    lane = lax.broadcasted_iota(jnp.int32, (rows, keys), 1)
    own_lane = lane - prompt_rows
    filled = jnp.zeros((rows, keys), jnp.int32)
    for s in range(seqs):
        filled = jnp.where(row_seq == s, lengths_ref[s], filled)
    slot = col * suffix_rows + own_lane % suffix_rows
    live = (lane < prompt_rows) | ((own_lane // suffix_rows == row_seq) & (slot < filled))

    def query_rows(start):
        first = queries_ref[:, pl.ds(start, HD)].astype(f32)
        second = queries_ref[:, pl.ds(start + HD, HD)].astype(f32)
        return jnp.concatenate([first, second], axis=0)

    def cached(which, head):
        lanes = slice(head * HD, (head + 1) * HD)
        suffix = suffix_ref[:, which, :, lanes].astype(f32).reshape(seqs * suffix_rows, HD)
        return jnp.concatenate([prompt_ref[0, which, :, lanes], suffix.astype(bf16)], axis=0)

    scores = []
    for head in range(col_count):
        scores.append(
            dot_nt(query_rows(2 * head * HD).astype(bf16), cached(0, head)) * score_scale
        )
    half = lax.broadcasted_iota(jnp.int32, (rows, HD), 1) < HD // 2
    for head in range(col_count):
        score = jnp.where(live, scores[head], neg_big)
        top = jnp.max(score, axis=1, keepdims=True).astype(bf16).astype(f32)
        weights = jnp.where(live, jnp.exp(score - top), 0.0)
        total = jnp.sum(weights, axis=1, keepdims=True)
        mixture = jnp.dot(weights.astype(bf16), cached(1, head), preferred_element_type=f32)
        part_out[head, 0:rows, :] = mixture.astype(bf16)
        part_out[head, rows : 2 * rows, :] = jnp.where(half, top, total).astype(bf16)

    pl.semaphore_wait(barrier, row_count + col_count - 2)
    send("col", col, col_count, 0, lambda peer: part_out.at[peer], lambda k: part_in.at[k])

    per_peer = experts * line_count // row_count
    block = move_out.shape[1]
    flat_lines = jnp.concatenate(
        [lines_ref[:, j].reshape(experts * line_count, width) for j in range(3)], axis=1
    )
    peers_at_once = 4
    chunk = peers_at_once * block
    send_slots = send_slot_ref[...]

    def sort_chunk(at, carry):
        wanted = at * chunk + lax.broadcasted_iota(jnp.int32, (chunk, experts * line_count), 0)
        picks = jnp.where(wanted == send_slots, 1.0, 0.0).astype(bf16)
        sorted_lines = jnp.dot(picks, flat_lines, preferred_element_type=f32).astype(bf16)
        move_out[pl.ds(at * peers_at_once, peers_at_once)] = sorted_lines.reshape(
            peers_at_once, block, 3 * width
        )
        return carry

    lax.fori_loop(0, row_count // peers_at_once, sort_chunk, 0)
    move_in[0] = move_out[row]
    send("row", row, row_count, 6, lambda peer: move_out.at[peer], lambda k: move_in.at[k])

    tail = line_count - 128
    for e in range(experts):
        lanes = slice(e * width, (e + 1) * width)
        wide[0:128, lanes] = lines_ref[e, 0, 0:128, :]
        wide[128:256, lanes] = lines_ref[e, 1, 0:128, :]
        wide[256 : 256 + tail, lanes] = lines_ref[e, 0, 128:line_count, :]
        wide[256 + tail : 256 + 2 * tail, lanes] = lines_ref[e, 1, 128:line_count, :]
        spare = 128 - 2 * tail
        router_row = jnp.broadcast_to(router_ref[e : e + 1, :].astype(f32), (spare, width))
        first = lax.broadcasted_iota(jnp.int32, (spare, width), 0) == 0
        wide[256 + 2 * tail : 384, lanes] = jnp.where(first, router_row, 0.0).astype(bf16)
        gap = jnp.zeros((64 - tail, width), bf16)
        down[e, 0:line_count, :] = lines_ref[e, 2]
        down[e, line_count : 128 + 64, :] = gap
        down[e, 192 : 192 + tail, :] = lines_ref[e, 2, 128:line_count, :]
        down[e, 192 + tail : 256, :] = gap

    part_in[0] = part_out[col]
    wait(col_count, 0, part_in, recv_sems)
    own_query = query_rows(pl.multiple_of(col * 2 * HD, 2 * HD))
    own_pair = new_kv_ref[:, :, pl.ds(pl.multiple_of(col * HD, HD), HD)].astype(f32)
    own_key = jnp.concatenate([own_pair[:, 0, :]] * 2, axis=0)
    own_value = jnp.concatenate([own_pair[:, 1, :]] * 2, axis=0)
    own_score = jnp.sum(own_query * own_key, axis=1, keepdims=True) * score_scale
    stats = part_in[:, rows : 2 * rows, :].astype(f32)
    top = jnp.maximum(jnp.max(stats, axis=0)[:, 0:1], own_score)
    own_weight = jnp.exp(own_score - top)
    mixture = own_weight.astype(bf16).astype(f32) * own_value
    total = jnp.zeros((rows, HD), f32)
    for k in range(col_count):
        factor = jnp.exp(stats[k][:, 0:1] - top)
        total = total + factor * stats[k]
        mixture = mixture + factor * part_in[k, 0:rows, :].astype(f32)
    total = total[:, HD // 2 : HD // 2 + 1] + own_weight
    heads_in[0] = (mixture / total).astype(bf16)
    send("col", col, col_count, 1, lambda peer: heads_in.at[0], lambda k: heads_in.at[k])

    wait(col_count, 1, heads_in, recv_sems)
    projected = jnp.zeros((rows, 2 * width), f32)
    for k in range(col_count):
        head = lax.rem(col + col_count - k, col_count)
        start = pl.multiple_of(head * 2 * HD, 2 * HD)
        pair = jnp.concatenate(
            [w_out_ref[pl.ds(start, HD), :], w_out_ref[pl.ds(start + HD, HD), :]], axis=1
        )
        projected = projected + jnp.dot(heads_in[k], pair, preferred_element_type=f32)
    projected = projected[0:seqs, 0:width] + projected[seqs:rows, width : 2 * width]
    h_float = (hidden_ref[...].astype(f32) + projected).astype(bf16).astype(f32)
    scaled = h_float * gain_ref[...].astype(f32)
    squares = jnp.sum(h_float * h_float, axis=1, keepdims=True)
    high = squares.astype(bf16).astype(f32)
    half = lax.broadcasted_iota(jnp.int32, (seqs, width), 1) < width // 2
    message = jnp.concatenate([scaled, jnp.where(half, high, squares - high)], axis=0).astype(bf16)
    token_out[0] = message
    token_in[row] = message
    send("row", row, row_count, 2, lambda peer: token_out.at[0], lambda k: token_in.at[row])

    routes = [jnp.broadcast_to(routes_ref[:, k : k + 1], (tokens, width)) for k in range(2)]
    wait(row_count, 2, token_in, recv_sems)
    everything = token_in[...].astype(f32)
    every_token = everything[:, 0:seqs, :].reshape(tokens, width)
    every_square = everything[:, seqs : 2 * seqs, :].reshape(tokens, width)
    square = every_square[:, 0:1] + every_square[:, width // 2 : width // 2 + 1]
    square_high = square.astype(bf16).astype(f32)
    token_lane = lax.broadcasted_iota(jnp.int32, (tokens, 128), 1)
    for k in range(2):
        masked = jnp.concatenate(
            [jnp.where(routes[k] == e, every_token, 0.0).astype(bf16) for e in range(experts)],
            axis=1,
        )
        picked = dot_nt(masked, wide[...])
        last = picked[:, 256:384]
        at = 2 * tail
        logit = last[:, at : at + 1]
        logit_high = logit.astype(bf16).astype(f32)
        last = jnp.where(token_lane == at + 1, logit - logit_high, last)
        last = jnp.where(token_lane == at + 2, square_high, last)
        last = jnp.where(token_lane == at + 3, square - square_high, last)
        picked = jnp.concatenate([picked[:, 0:256], last], axis=1)
        summed_out[:, k] = picked.reshape(col_count, share, 384).astype(bf16)
    send("col", col, col_count, 3, lambda peer: summed_out.at[peer], lambda k: summed_in.at[k])

    summed_in[0] = summed_out[col]
    wait(col_count, 3, summed_in, recv_sems)
    sums = jnp.zeros((2, share, 384), f32)
    for k in range(col_count):
        sums = sums + summed_in[k].astype(f32)
    last = sums[:, :, 256:384]
    at = 2 * tail
    square = last[:, :, at + 2 : at + 3] + last[:, :, at + 3 : at + 4]
    inverse_rms = lax.rsqrt(square / (width * col_count) + norm_eps)
    logits = (last[:, :, at : at + 1] + last[:, :, at + 1 : at + 2]) * inverse_rms
    logits = jnp.exp(logits - jnp.max(logits, axis=0, keepdims=True))
    gates = logits / jnp.sum(logits, axis=0, keepdims=True)
    last = last.reshape(2 * share, 128)
    shifted = pltpu.roll(last, 128 - tail, 1).reshape(2, share, 128)
    last = last.reshape(2, share, 128)

    def activated(gate, up):
        gate = gate * inverse_rms
        return gate / (1.0 + jnp.exp(-gate)) * (up * inverse_rms) * gates

    act_first = activated(sums[:, :, 0:128], sums[:, :, 128:256])
    act_last = activated(last, shifted)
    share_lane = lax.broadcasted_iota(jnp.int32, (share, 128), 1)
    second = pltpu.roll(act_last[1], 64, 1)
    ends = jnp.where(
        share_lane < tail,
        act_last[0],
        jnp.where((share_lane >= 64) & (share_lane < 64 + tail), second, 0.0),
    )
    message = jnp.concatenate([act_first[0], act_first[1], ends], axis=0).astype(bf16)
    message = message.reshape(3, share, 128)
    act_out[0] = message
    act_in[col] = message
    send("col", col, col_count, 4, lambda peer: act_out.at[0], lambda k: act_in.at[col])

    wait(col_count, 4, act_in, recv_sems)
    firsts = [act_in[:, k].reshape(tokens, 128).astype(f32) for k in range(2)]
    ends = act_in[:, 2].reshape(tokens, 128).astype(f32)
    end_route = jnp.where(token_lane < 64, routes[0], routes[1])
    mixed = jnp.zeros((tokens, width), f32)
    for e in range(experts):
        begin = jnp.where(routes[0] == e, firsts[0], jnp.where(routes[1] == e, firsts[1], 0.0))
        end = jnp.where(end_route == e, ends, 0.0)
        both = jnp.concatenate([begin, end], axis=1).astype(bf16)
        mixed = mixed + jnp.dot(both, down[e], preferred_element_type=f32)
    mixed_out[...] = mixed.reshape(row_count, seqs, width).astype(bf16)
    send("row", row, row_count, 5, lambda peer: mixed_out.at[peer], lambda k: mixed_in.at[k])
    mixed_in[0] = mixed_out[row]
    wait(row_count, 5, mixed_in, recv_sems)
    layer_ref[...] = h_float + jnp.sum(mixed_in[...].astype(f32), axis=0)

    wait(row_count, 6, move_in, recv_sems)
    everything = move_in[...].reshape(row_count * block, 3 * width)

    def place(e, carry):
        slots = take_slot_ref[pl.ds(pl.multiple_of(e * line_count, line_count), line_count), :]
        held = lax.broadcasted_iota(jnp.int32, (line_count, row_count * block), 1)
        picks = jnp.where(held == slots, 1.0, 0.0).astype(bf16)
        placed = jnp.dot(picks, everything, preferred_element_type=f32).astype(bf16)
        for j in range(3):
            moved_ref[e, j] = placed[:, j * width : (j + 1) * width]
        return carry

    lax.fori_loop(0, experts, place, 0)

    wait(col_count, 0, part_in, send_sems)
    wait(col_count, 1, heads_in, send_sems)
    wait(row_count, 2, token_in, send_sems)
    wait(col_count, 3, summed_in, send_sems)
    wait(col_count, 4, act_in, send_sems)
    wait(row_count, 5, mixed_in, send_sems)
    wait(row_count, 6, move_in, send_sems)


def owner_slots(ids, table, block, per_peer):
    experts, full = table.shape
    lines = ids.shape[1]
    owners = jnp.arange(full, dtype=jnp.int32) // lines
    owner = jnp.sum(
        jnp.where(ids[:, :, None] == table[:, None, :], owners[None, None, :], 0), axis=2
    )
    keys = owner * (experts * full) + jnp.arange(experts, dtype=jnp.int32)[:, None] * full + ids
    owner, keys = owner.reshape(-1), keys.reshape(-1)
    place = jnp.sum((keys[None, :] < keys[:, None]).astype(jnp.int32), axis=1)
    return owner, place + owner * (block - per_peer)


def local(
    row_count,
    col_count,
    hidden,
    queries,
    new_kv,
    prompt_kv,
    suffix_kv,
    lengths,
    w_out,
    moe_gain,
    w_router,
    expert_weights,
    old_lines,
    new_lines,
    routes,
):
    experts, line_count, parts, width = expert_weights.shape
    seqs = hidden.shape[0]
    tokens = seqs * row_count
    share = tokens // col_count
    per_peer = experts * line_count // row_count
    block = rounded_up(per_peer, 16)
    row = lax.axis_index("row")
    held = lax.dynamic_slice_in_dim(old_lines, row * line_count, line_count, 1)
    wanted = lax.dynamic_slice_in_dim(new_lines, row * line_count, line_count, 1)
    _, send_slots = owner_slots(held, new_lines, block, per_peer)
    source, place = owner_slots(wanted, old_lines, block, per_peer)
    distance = lax.rem(row + row_count - source, row_count)
    take_slots = place + (distance - source) * block
    vmem = pl.BlockSpec(memory_space=pltpu.VMEM)
    rows = 2 * seqs
    layer_out, moved = pl.pallas_call(
        functools.partial(step_kernel, row_count, col_count),
        out_shape=(
            jax.ShapeDtypeStruct((seqs, width), f32),
            jax.ShapeDtypeStruct((experts, parts, line_count, width), bf16),
        ),
        in_specs=[pl.BlockSpec(memory_space=pltpu.SMEM)] + [vmem] * 12,
        out_specs=(vmem, vmem),
        scratch_shapes=[
            pltpu.VMEM((col_count, 2 * rows, HD), bf16),
            pltpu.VMEM((col_count, 2 * rows, HD), bf16),
            pltpu.VMEM((col_count, rows, HD), bf16),
            pltpu.VMEM((1, rows, width), bf16),
            pltpu.VMEM((row_count, rows, width), bf16),
            pltpu.VMEM((384, experts * width), bf16),
            pltpu.VMEM((col_count, 2, share, 384), bf16),
            pltpu.VMEM((col_count, 2, share, 384), bf16),
            pltpu.VMEM((1, 3, share, 128), bf16),
            pltpu.VMEM((col_count, 3, share, 128), bf16),
            pltpu.VMEM((experts, 256, width), bf16),
            pltpu.VMEM((row_count, seqs, width), bf16),
            pltpu.VMEM((row_count, seqs, width), bf16),
            pltpu.VMEM((row_count, block, parts * width), bf16),
            pltpu.VMEM((row_count, block, parts * width), bf16),
            pltpu.SemaphoreType.DMA((7,)),
            pltpu.SemaphoreType.DMA((7,)),
        ],
        compiler_params=pltpu.CompilerParams(
            collective_id=0, has_side_effects=True, vmem_limit_bytes=56 << 20
        ),
        name="decode_step",
    )(
        lengths,
        hidden,
        queries,
        new_kv,
        prompt_kv,
        suffix_kv,
        w_out,
        moe_gain.reshape(1, width),
        jnp.transpose(w_router),
        jnp.transpose(expert_weights, (0, 2, 1, 3)),
        send_slots.reshape(1, -1),
        take_slots.reshape(-1, 1),
        routes,
    )
    return layer_out, jnp.transpose(moved, (0, 2, 1, 3))


def solution(mesh):
    return jax.shard_map(
        functools.partial(local, mesh.shape["row"], mesh.shape["col"]),
        mesh=mesh,
        in_specs=(
            P("row", "col"),
            P("row", None),
            P("row", None, None),
            P("row", None, "col", None),
            P("row", None, "col", None),
            P("row"),
            P(None, "col"),
            P("col"),
            P("col", None),
            P(None, "row", None, "col"),
            P(),
            P(),
            P(),
        ),
        out_specs=(P("row", "col"), P(None, "row", None, "col")),
        check_vma=False,
    )
```

time: 1100 us -> 146 us (0.13)
  local copies, waits for them, and re-layouts: 415 us -> 6.36 us
  waiting for transfers between devices: 358 us -> 0 us
  blocking collectives: 251 us -> 0 us
  Pallas kernels: 0 us -> 126 us
  other arithmetic: 33.2 us -> 12.8 us
  starting transfers between devices: 19.6 us -> 0 us
  between operations: 15.8 us -> 0.7 us
    unnamed x52 -> x3, local copies, waits for them, and re-layouts: 336 us -> 5.03 us
    unnamed x4 -> x0, waiting for transfers between devices: 322 us -> none
    all_gather x3 -> x0, blocking collectives: 133 us -> none  [the longest x1 68.4 us: local(): lax.all_gather(scaled, 'row', axis=0, tiled=True)]
    pallas_call x0 -> x1, Pallas kernels: none -> 126 us  [local(): pl.pallas_call(functools.partial(step_kernel, row_count, col_count), out_...]
    unnamed x1 -> x0, blocking collectives: 83.8 us -> none
    gather x11 -> x0, local copies, waits for them, and re-layouts: 37.1 us -> none  [the longest x3 8.72 us: migrate(): target_slots = jnp.take_along_axis(inverse_new, held_ids, axis=1)]
    psum x1 -> x0, waiting for transfers between devices: 36.3 us -> none  [local(): lax.psum((picked, router_part, every_square), 'col')]
    psum x1 -> x0, blocking collectives: 33.7 us -> none  [local(): lax.psum((picked, router_part, every_square), 'col')]
  transfers between devices with their start and end apart: 4 -> 0, of which waited for: 2 -> 0; matrix products, arithmetic and copies ran while one was open for 41% -> 0% of each run, Pallas kernels for 0% -> 0%
where the time goes in v1:
time: 146 us
  Pallas kernels  126 us (86%)
  other arithmetic  12.8 us (9%)
  local copies, waits for them, and re-layouts  6.36 us (4%)
    pallas_call x1, Pallas kernels, local(): pl.pallas_call(functools.partial(step_kernel, row_count, col_count), out_...  126 us
    reduce_sum x1, other arithmetic, owner_slots(): jnp.sum(jnp.where(ids[:, :, None] == table[:, None, :], owners[None, None...  9.06 us
    unnamed x3, local copies, waits for them, and re-layouts  5.03 us

profile of v1, /device:TPU:1, one launch (start us, length us, event | category | flops | bytes accessed | tf_op | source)
XLA Modules:
  0.0 145.5 jit_solution(12780063197869535859)
XLA Ops:
  0.6 0.8 constant_dynamic-slice_fusion
  1.5 9.1 %select_reduce_fusion = (s32[8,176]{1,0:T(8,128)S(1)}, s32[8,176]{1,0:T(8,128)S(1)}) fusion(s32[8,5632]{1,0:T(8,128)} %param.23, s32[8,176]{1,0:T(8,128)S(1)} %get-tuple-element.11, s32[5632]{0:T(1024)S(1)} %add_select_fusion, s32[8,5632]{1,0:T(8,128)} %param.24, s32[8,176]{1,0:T(8,128)S(1)} %get-tuple-element.12), kind=kLoop, calls=%fused_computation | loop fusion | flops 47576320 | bytes 405504 | tf_op jit(solution)/shard_map/reduce_sum | solution.py:326
  10.5 0.1 add_add_fusion.1
  10.6 0.1 lt.35
  10.7 0.9 convert_reduce_fusion.1
  11.6 0.1 mul.61
  11.7 0.6 reshape_add_fusion.1.send_slot_ref
  12.3 0.1 lt.39
  12.4 0.9 convert_reduce_fusion
  13.3 1.5 %copy.31.routes_ref = s32[256,2]{1,0:T(8,128)} copy(s32[256,2]{0,1:T(2,128)} %param.25) | data formatting | bytes 4096 | tf_op args[12]
  14.8 0.3 reshape.119
  15.1 1.2 fusion.3.take_slot_ref
  16.3 125.7 %decode_step.1 = (f32[8,128]{1,0:T(8,128)}, bf16[8,3,176,128]{3,2,1,0:T(8,128)(2,1)}) custom-call(s32[8]{0:T(128)} %lengths_ref.1, bf16[8,128]{1,0:T(8,128)(2,1)} %hidden_ref.1, bf16[8,4096]{1,0:T(8,128)(2,1)} %queries_ref.1, bf16[8,2,2048]{2,1,0:T(2,128)(2,1)} %new_kv_ref.1, bf16[1,2,64,2048]{3,2,1,0:T(8,128)(2,1)} %prompt_ref.1, ...), custom_call_target="tpu_custom_call" | custom-call | tf_op jit(solution)/shard_map/decode_step/pallas_call | solution.py:367
  142.0 1.3 copy.34
  143.3 2.3 %copy.35 = bf16[8,176,3,128]{3,1,2,0:T(8,128)(2,1)} copy(bf16[8,176,3,128]{3,1,2,0:T(8,128)(2,1)} %bitcast.4) | data formatting | bytes 2162688
  (2 shorter events, 0.0 us)

commit v2 on v1

v2 whole, which is shorter than its diff:
```python
import functools

import jax
import jax.numpy as jnp
from jax import lax
from jax.experimental import pallas as pl
from jax.experimental.pallas import tpu as pltpu
from jax.sharding import PartitionSpec as P

HD = 128
norm_eps = 1e-06
neg_big = -1e30
f32 = jnp.float32
bf16 = jnp.bfloat16
MESH = pl.DeviceIdType.MESH
MOVES = (0, 3, 6, 9, 12, 15, 18, 21, 24, 27, 29, 31)


def rounded_up(value, step):
    return (value + step - 1) // step * step


def dot_nt(a, b):
    return lax.dot_general(a, b, (((1,), (1,)), ((), ())), preferred_element_type=f32)


def split(count):
    far = 4 if count >= 16 else 2
    return far, count // far


def line_slots(row, row_count, block, ids_ref, table_ref, line_count, outgoing):
    experts, full = table_ref.shape
    window = min(full, 512)
    start = row * line_count
    base = jnp.minimum(start // 128 * 128, full - window)
    held = ids_ref[:, pl.ds(pl.multiple_of(base, 128), window)]
    held = pltpu.roll(held, lax.rem(window - (start - base), window), 1)[:, 0:256]
    id_rows = held.astype(f32)
    padded = jnp.concatenate([id_rows, jnp.zeros((128 - experts, 256), f32)], axis=0)
    id_columns = jnp.transpose(padded)[0:line_count]
    owner_lane = lax.broadcasted_iota(jnp.int32, (1, 128), 1)
    owners_f32 = owner_lane.astype(f32)
    if outgoing:
        offsets = owners_f32 * block
    else:
        far_count, near_count = split(row_count)
        far = lax.rem(row // near_count - owner_lane // near_count + 128 * far_count, far_count)
        near = lax.rem(row % near_count - owner_lane % near_count + near_count, near_count)
        offsets = (near * far_count + far).astype(f32) * block
    counts = jnp.zeros((1, 128), f32)
    slots = []
    for e in range(experts):
        id_column = id_columns[:, e : e + 1]
        wanted = jnp.broadcast_to(id_column, (line_count, 128)).astype(jnp.int32)

        def search(chunk, found):
            at = chunk * 128
            table = table_ref[e : e + 1, pl.ds(pl.multiple_of(at, 128), 128)]
            first = at // line_count
            owner = first + jnp.where(owner_lane + at >= (first + 1) * line_count, 1, 0)
            return jnp.where(wanted == table, owner, found)

        found = lax.fori_loop(
            0, full // 128, search, jnp.zeros((line_count, 128), jnp.int32), unroll=4
        )
        owner_column = jnp.sum(found.astype(f32), axis=1, keepdims=True)
        hits = jnp.where(owner_column == owners_f32, 1.0, 0.0)
        pack = jnp.concatenate([counts, offsets, owners_f32, jnp.zeros((5, 128), f32)], axis=0)
        looked = dot_nt(pack.astype(bf16), hits.astype(bf16))
        owner_row = looked[2:3]
        id_row = id_rows[e : e + 1, 0:line_count]
        same = owner_column == owner_row
        if outgoing:
            rank = jnp.sum(jnp.where(same & (id_column < id_row), 1.0, 0.0), axis=0, keepdims=True)
            slots.append(rank + looked[0:1] + looked[1:2])
        else:
            rank = jnp.sum(jnp.where(same & (id_row < id_column), 1.0, 0.0), axis=1, keepdims=True)
            slots.append(rank + jnp.sum(hits * (counts + offsets), axis=1, keepdims=True))
        counts = counts + jnp.sum(hits, axis=0, keepdims=True)
    return slots


def step_kernel(
    row_count,
    col_count,
    lengths_ref,
    hidden_ref,
    queries_ref,
    new_kv_ref,
    prompt_ref,
    suffix_ref,
    w_out_ref,
    gain_ref,
    router_ref,
    lines_ref,
    old_lines_ref,
    new_lines_ref,
    routes_ref,
    layer_ref,
    moved_ref,
    part_out,
    part_in,
    joined_out,
    joined_in,
    heads_in,
    token_in,
    wide,
    summed_out,
    summed_in,
    halved_out,
    halved_in,
    act_in,
    down,
    mixed_out,
    mixed_in,
    nearer_out,
    nearer_in,
    move_out,
    move_in,
    take_slots,
    send_sems,
    recv_sems,
):
    row = lax.axis_index("row")
    col = lax.axis_index("col")
    seqs = hidden_ref.shape[0]
    experts, _, line_count, width = lines_ref.shape
    prompt_rows = prompt_ref.shape[2]
    suffix_rows = suffix_ref.shape[2]
    tokens = seqs * row_count
    share = tokens // col_count
    score_scale = HD ** (-0.5)

    barrier = pltpu.get_barrier_semaphore()
    row_far_count, row_near_count = split(row_count)
    col_far_count, col_near_count = split(col_count)
    row_far, row_near = row // row_near_count, row % row_near_count
    col_far, col_near = col // col_near_count, col % col_near_count

    def col_far_peer(k):
        far = lax.rem(col_far + k, col_far_count)
        return far, {"col": far * col_near_count + col_near}

    def col_near_peer(k):
        near = lax.rem(col_near + k, col_near_count)
        return near, {"col": col_far * col_near_count + near}

    def row_far_peer(k):
        far = lax.rem(row_far + k, row_far_count)
        return far, {"row": far * row_near_count + row_near}

    def row_near_peer(k):
        near = lax.rem(row_near + k, row_near_count)
        return near, {"row": row_far * row_near_count + near}

    def row_peer(k):
        far = lax.rem(row_far + k % row_far_count, row_far_count)
        near = lax.rem(row_near + k // row_far_count, row_near_count)
        peer = far * row_near_count + near
        return peer, {"row": peer}

    def greet(peer_of, count):
        def body(k, carry):
            pl.semaphore_signal(barrier, inc=1, device_id=peer_of(k)[1], device_id_type=MESH)
            return carry

        lax.fori_loop(1, count, body, 0)

    greet(col_far_peer, col_far_count)
    greet(col_near_peer, col_near_count)
    greet(row_peer, row_count)
    greeted = col_far_count + col_near_count + row_count - 3

    def send(peer_of, first, last, lane, source, target):
        def body(k, carry):
            peer, device = peer_of(k)
            pltpu.make_async_remote_copy(
                src_ref=source(peer),
                dst_ref=target(k),
                send_sem=send_sems.at[lane],
                recv_sem=recv_sems.at[lane],
                device_id=device,
                device_id_type=MESH,
            ).start()
            return carry

        lax.fori_loop(first, last, body, 0)

    def wait(lane, copies, sems):
        pltpu.make_async_copy(copies, copies, sems.at[lane]).wait()

    rows = 2 * seqs
    keys = prompt_rows + seqs * suffix_rows
    row_seq = lax.broadcasted_iota(jnp.int32, (rows, keys), 0) % seqs
    lane = lax.broadcasted_iota(jnp.int32, (rows, keys), 1)
    own_lane = lane - prompt_rows
    filled = jnp.zeros((rows, keys), jnp.int32)
    for s in range(seqs):
        filled = jnp.where(row_seq == s, lengths_ref[s], filled)
    slot = col * suffix_rows + own_lane % suffix_rows
    live = (lane < prompt_rows) | ((own_lane // suffix_rows == row_seq) & (slot < filled))

    def query_rows(start):
        first = queries_ref[:, pl.ds(start, HD)].astype(f32)
        second = queries_ref[:, pl.ds(start + HD, HD)].astype(f32)
        return jnp.concatenate([first, second], axis=0)

    def cached(which, head):
        lanes = slice(head * HD, (head + 1) * HD)
        suffix = suffix_ref[:, which, :, lanes].astype(f32).reshape(seqs * suffix_rows, HD)
        return jnp.concatenate([prompt_ref[0, which, :, lanes], suffix.astype(bf16)], axis=0)

    scores = []
    for head in range(col_count):
        scores.append(
            dot_nt(query_rows(2 * head * HD).astype(bf16), cached(0, head)) * score_scale
        )
    half = lax.broadcasted_iota(jnp.int32, (rows, HD), 1) < HD // 2
    for head in range(col_count):
        score = jnp.where(live, scores[head], neg_big)
        top = jnp.max(score, axis=1, keepdims=True).astype(bf16).astype(f32)
        weights = jnp.where(live, jnp.exp(score - top), 0.0)
        total = jnp.sum(weights, axis=1, keepdims=True)
        mixture = jnp.dot(weights.astype(bf16), cached(1, head), preferred_element_type=f32)
        near, far = head % col_near_count, head // col_near_count
        part_out[near, far, 0:rows, :] = mixture.astype(bf16)
        part_out[near, far, rows : 2 * rows, :] = jnp.where(half, top, total).astype(bf16)

    pl.semaphore_wait(barrier, greeted)
    near_parts = part_in.at[pl.ds(1, col_near_count - 1)]
    send(
        col_near_peer,
        1,
        col_near_count,
        0,
        lambda peer: part_out.at[peer],
        lambda k: part_in.at[k],
    )

    per_peer = experts * line_count // row_count
    block = move_out.shape[1]
    slots = line_slots(row, row_count, block, old_lines_ref, new_lines_ref, line_count, True)
    peers_at_once = 4
    chunk = peers_at_once * block

    def sort_chunk(at, carry):
        wanted = (
            at * chunk + lax.broadcasted_iota(jnp.int32, (chunk, line_count), 0)
        ).astype(f32)
        sorted_lines = jnp.zeros((chunk, 3 * width), f32)
        for e in range(experts):
            picks = jnp.where(wanted == slots[e], 1.0, 0.0).astype(bf16)
            lines = jnp.concatenate([lines_ref[e, j] for j in range(3)], axis=1)
            sorted_lines = sorted_lines + jnp.dot(picks, lines, preferred_element_type=f32)
        move_out[pl.ds(at * peers_at_once, peers_at_once)] = (
            sorted_lines.astype(bf16).reshape(peers_at_once, block, 3 * width)
        )
        return carry

    moves = [1 + (row_count - 1) * share_of // 31 for share_of in MOVES]

    def move(batch):
        send(
            row_peer,
            moves[batch],
            moves[batch + 1],
            12,
            lambda peer: move_out.at[peer],
            lambda k: move_in.at[k],
        )

    def join(parts, tops):
        top = tops[0]
        for other in tops[1:]:
            top = jnp.maximum(top, other)
        total = jnp.zeros((rows, HD), f32)
        mixture = jnp.zeros((rows, HD), f32)
        for part in parts:
            stats = part[rows : 2 * rows].astype(f32)
            factor = jnp.exp(stats[:, 0:1] - top)
            total = total + factor * stats
            mixture = mixture + factor * part[0:rows].astype(f32)
        return top, total[:, HD // 2 : HD // 2 + 1], mixture

    def top_of(part):
        return part[rows : 2 * rows].astype(f32)[:, 0:1]

    part_in[0] = part_out[col_near]
    wait(0, near_parts, recv_sems)
    for far in range(col_far_count):
        parts = [part_in[k, far] for k in range(col_near_count)]
        top, total, mixture = join(parts, [top_of(part) for part in parts])
        joined_out[far, 0:rows, :] = mixture.astype(bf16)
        joined_out[far, rows : 2 * rows, :] = jnp.where(half, top, total).astype(bf16)
    far_parts = joined_in.at[pl.ds(1, col_far_count - 1)]
    send(
        col_far_peer,
        1,
        col_far_count,
        1,
        lambda peer: joined_out.at[peer],
        lambda k: joined_in.at[k],
    )
    lax.fori_loop(0, row_count // peers_at_once, sort_chunk, 0)
    move_in[0] = move_out[row]
    move(0)

    joined_in[0] = joined_out[col_far]
    own_query = query_rows(pl.multiple_of(col * 2 * HD, 2 * HD))
    own_pair = new_kv_ref[:, :, pl.ds(pl.multiple_of(col * HD, HD), HD)].astype(f32)
    own_key = jnp.concatenate([own_pair[:, 0, :]] * 2, axis=0)
    own_value = jnp.concatenate([own_pair[:, 1, :]] * 2, axis=0)
    own_score = jnp.sum(own_query * own_key, axis=1, keepdims=True) * score_scale
    wait(1, far_parts, recv_sems)
    parts = [joined_in[k] for k in range(col_far_count)]
    top, total, mixture = join(parts, [top_of(part) for part in parts] + [own_score])
    own_weight = jnp.exp(own_score - top)
    mixture = mixture + own_weight.astype(bf16).astype(f32) * own_value
    heads_in[0, col_far] = (mixture / (total + own_weight)).astype(bf16)
    own_heads = heads_in.at[0, col_far]
    far_heads = heads_in.at[0, pl.ds(0, col_far_count - 1)]
    near_heads = heads_in.at[pl.ds(1, col_near_count - 1)]
    send(col_far_peer, 1, col_far_count, 2, lambda peer: own_heads, lambda k: own_heads)
    move(1)

    tail = line_count - 128
    for e in range(experts):
        lanes = slice(e * width, (e + 1) * width)
        wide[0:128, lanes] = lines_ref[e, 0, 0:128, :]
        wide[128:256, lanes] = lines_ref[e, 1, 0:128, :]
        wide[256 : 256 + tail, lanes] = lines_ref[e, 0, 128:line_count, :]
        wide[256 + tail : 256 + 2 * tail, lanes] = lines_ref[e, 1, 128:line_count, :]
        spare = 128 - 2 * tail
        router_row = jnp.broadcast_to(router_ref[e : e + 1, :].astype(f32), (spare, width))
        first = lax.broadcasted_iota(jnp.int32, (spare, width), 0) == 0
        wide[256 + 2 * tail : 384, lanes] = jnp.where(first, router_row, 0.0).astype(bf16)
        gap = jnp.zeros((64 - tail, width), bf16)
        down[e, 0:line_count, :] = lines_ref[e, 2]
        down[e, line_count : 128 + 64, :] = gap
        down[e, 192 : 192 + tail, :] = lines_ref[e, 2, 128:line_count, :]
        down[e, 192 + tail : 256, :] = gap

    wait(2, far_heads, recv_sems)
    send(
        col_near_peer,
        1,
        col_near_count,
        3,
        lambda peer: heads_in.at[0],
        lambda k: heads_in.at[k],
    )
    move(2)
    wait(3, near_heads, recv_sems)
    projected = jnp.zeros((rows, 2 * width), f32)
    for k in range(col_near_count):
        near = lax.rem(col_near + col_near_count - k, col_near_count)
        for far in range(col_far_count):
            head = far * col_near_count + near
            start = pl.multiple_of(head * 2 * HD, 2 * HD)
            pair = jnp.concatenate(
                [w_out_ref[pl.ds(start, HD), :], w_out_ref[pl.ds(start + HD, HD), :]], axis=1
            )
            projected = projected + jnp.dot(heads_in[k, far], pair, preferred_element_type=f32)
    projected = projected[0:seqs, 0:width] + projected[seqs:rows, width : 2 * width]
    h_float = (hidden_ref[...].astype(f32) + projected).astype(bf16).astype(f32)
    scaled = h_float * gain_ref[...].astype(f32)
    squares = jnp.sum(h_float * h_float, axis=1, keepdims=True)
    high = squares.astype(bf16).astype(f32)
    half = lax.broadcasted_iota(jnp.int32, (seqs, width), 1) < width // 2
    message = jnp.concatenate([scaled, jnp.where(half, high, squares - high)], axis=0).astype(bf16)
    token_in[row_near, row_far] = message
    own_tokens = token_in.at[row_near, row_far]
    far_tokens = token_in.at[0, pl.ds(0, row_far_count - 1)]
    near_tokens = token_in.at[pl.ds(0, row_near_count - 1)]
    send(row_far_peer, 1, row_far_count, 4, lambda peer: own_tokens, lambda k: own_tokens)
    move(3)

    for e, slots in enumerate(
        line_slots(row, row_count, block, new_lines_ref, old_lines_ref, line_count, False)
    ):
        take_slots[e] = jnp.broadcast_to(slots, (line_count, 128))
    routes = [
        jnp.transpose(jnp.broadcast_to(routes_ref[k : k + 1, :].astype(f32), (width, tokens)))
        for k in range(2)
    ]

    wait(4, far_tokens, recv_sems)
    own_tokens = token_in.at[row_near]
    send(row_near_peer, 1, row_near_count, 5, lambda peer: own_tokens, lambda k: own_tokens)
    move(4)
    wait(5, near_tokens, recv_sems)
    everything = token_in[...].astype(f32)
    by_row = [everything[r % row_near_count, r // row_near_count] for r in range(row_count)]
    every_token = jnp.concatenate([part[0:seqs] for part in by_row], axis=0)
    every_square = jnp.concatenate([part[seqs : 2 * seqs] for part in by_row], axis=0)
    square = every_square[:, 0:1] + every_square[:, width // 2 : width // 2 + 1]
    token_lane = lax.broadcasted_iota(jnp.int32, (tokens, 128), 1)
    at = 2 * tail

    def with_spares(last, logit, square):
        spare = lax.broadcasted_iota(jnp.int32, last.shape, len(last.shape) - 1) - at
        logit_high = logit.astype(bf16).astype(f32)
        square_high = square.astype(bf16).astype(f32)
        last = jnp.where(spare == 0, logit_high, last)
        last = jnp.where(spare == 1, logit - logit_high, last)
        last = jnp.where(spare == 2, square_high, last)
        return jnp.where(spare == 3, square - square_high, last)

    for k in range(2):
        masked = jnp.concatenate(
            [jnp.where(routes[k] == e, every_token, 0.0).astype(bf16) for e in range(experts)],
            axis=1,
        )
        picked = dot_nt(masked, wide[...])
        last = picked[:, 256:384]
        last = with_spares(last, last[:, at : at + 1], square)
        picked = jnp.concatenate([picked[:, 0:256], last], axis=1).astype(bf16)
        for c in range(col_count):
            summed_out[c % col_near_count, c // col_near_count, k] = picked[
                c * share : (c + 1) * share
            ]
    near_sums = summed_in.at[pl.ds(1, col_near_count - 1)]
    far_sums = halved_in.at[pl.ds(1, col_far_count - 1)]
    send(
        col_near_peer,
        1,
        col_near_count,
        6,
        lambda peer: summed_out.at[peer],
        lambda k: summed_in.at[k],
    )
    move(5)

    summed_in[0] = summed_out[col_near]
    wait(6, near_sums, recv_sems)
    for far in range(col_far_count):
        sums = summed_in[0, far].astype(f32)
        for k in range(1, col_near_count):
            sums = sums + summed_in[k, far].astype(f32)
        last = sums[:, :, 256:384]
        logit = last[:, :, at : at + 1] + last[:, :, at + 1 : at + 2]
        square = last[:, :, at + 2 : at + 3] + last[:, :, at + 3 : at + 4]
        halved_out[far, :, :, 0:256] = sums[:, :, 0:256].astype(bf16)
        halved_out[far, :, :, 256:384] = with_spares(last, logit, square).astype(bf16)
    send(
        col_far_peer,
        1,
        col_far_count,
        7,
        lambda peer: halved_out.at[peer],
        lambda k: halved_in.at[k],
    )
    move(6)
    halved_in[0] = halved_out[col_far]
    wait(7, far_sums, recv_sems)
    sums = halved_in[0].astype(f32)
    for k in range(1, col_far_count):
        sums = sums + halved_in[k].astype(f32)
    last = sums[:, :, 256:384]
    square = last[:, :, at + 2 : at + 3] + last[:, :, at + 3 : at + 4]
    inverse_rms = lax.rsqrt(square / (width * col_count) + norm_eps)
    logits = (last[:, :, at : at + 1] + last[:, :, at + 1 : at + 2]) * inverse_rms
    logits = jnp.exp(logits - jnp.max(logits, axis=0, keepdims=True))
    gates = logits / jnp.sum(logits, axis=0, keepdims=True)
    last = last.reshape(2 * share, 128)
    shifted = pltpu.roll(last, 128 - tail, 1).reshape(2, share, 128)
    last = last.reshape(2, share, 128)

    def activated(gate, up):
        gate = gate * inverse_rms
        return gate / (1.0 + jnp.exp(-gate)) * (up * inverse_rms) * gates

    act_first = activated(sums[:, :, 0:128], sums[:, :, 128:256])
    act_last = activated(last, shifted)
    share_lane = lax.broadcasted_iota(jnp.int32, (share, 128), 1)
    second = pltpu.roll(act_last[1], 64, 1)
    ends = jnp.where(
        share_lane < tail,
        act_last[0],
        jnp.where((share_lane >= 64) & (share_lane < 64 + tail), second, 0.0),
    )
    message = jnp.concatenate([act_first[0], act_first[1], ends], axis=0).astype(bf16)
    act_in[col_near, col_far] = message.reshape(3, share, 128)
    own_acts = act_in.at[col_near, col_far]
    far_acts = act_in.at[0, pl.ds(0, col_far_count - 1)]
    near_acts = act_in.at[pl.ds(0, col_near_count - 1)]
    send(col_far_peer, 1, col_far_count, 8, lambda peer: own_acts, lambda k: own_acts)
    move(7)
    wait(8, far_acts, recv_sems)
    own_row = act_in.at[col_near]
    send(col_near_peer, 1, col_near_count, 9, lambda peer: own_row, lambda k: own_row)
    move(8)

    wait(9, near_acts, recv_sems)
    by_col = [act_in[c % col_near_count, c // col_near_count] for c in range(col_count)]
    firsts = [
        jnp.concatenate([part[k] for part in by_col], axis=0).astype(f32) for k in range(2)
    ]
    ends = jnp.concatenate([part[2] for part in by_col], axis=0).astype(f32)
    end_route = jnp.where(token_lane < 64, routes[0], routes[1])
    mixed = jnp.zeros((tokens, width), f32)
    for e in range(experts):
        begin = jnp.where(routes[0] == e, firsts[0], jnp.where(routes[1] == e, firsts[1], 0.0))
        end = jnp.where(end_route == e, ends, 0.0)
        both = jnp.concatenate([begin, end], axis=1).astype(bf16)
        mixed = mixed + jnp.dot(both, down[e], preferred_element_type=f32)
    for r in range(row_count):
        mixed_out[r % row_near_count, r // row_near_count] = mixed[
            r * seqs : (r + 1) * seqs
        ].astype(bf16)
    near_mixed = mixed_in.at[pl.ds(1, row_near_count - 1)]
    far_mixed = nearer_in.at[pl.ds(1, row_far_count - 1)]
    send(
        row_near_peer,
        1,
        row_near_count,
        10,
        lambda peer: mixed_out.at[peer],
        lambda k: mixed_in.at[k],
    )
    move(9)
    mixed_in[0] = mixed_out[row_near]
    wait(10, near_mixed, recv_sems)
    nearer_out[...] = jnp.sum(mixed_in[...].astype(f32), axis=0).astype(bf16)
    send(
        row_far_peer,
        1,
        row_far_count,
        11,
        lambda peer: nearer_out.at[peer],
        lambda k: nearer_in.at[k],
    )
    move(10)
    nearer_in[0] = nearer_out[row_far]
    wait(11, far_mixed, recv_sems)
    layer_ref[...] = h_float + jnp.sum(nearer_in[...].astype(f32), axis=0)

    moved = move_in.at[pl.ds(1, row_count - 1)]
    wait(12, moved, recv_sems)
    everything = move_in[...].reshape(row_count * block, 3 * width)

    def place(e, carry):
        slots = take_slots[e][:, 0:1]
        held = lax.broadcasted_iota(jnp.int32, (line_count, row_count * block), 1).astype(f32)
        picks = jnp.where(held == slots, 1.0, 0.0).astype(bf16)
        placed = jnp.dot(picks, everything, preferred_element_type=f32).astype(bf16)
        for j in range(3):
            moved_ref[e, j] = placed[:, j * width : (j + 1) * width]
        return carry

    lax.fori_loop(0, experts, place, 0)

    sent = [near_parts, far_parts, far_heads, near_heads, far_tokens, near_tokens, near_sums]
    sent += [far_sums, far_acts, near_acts, near_mixed, far_mixed, moved]
    for lane, copies in enumerate(sent):
        wait(lane, copies, send_sems)


def local(
    row_count,
    col_count,
    hidden,
    queries,
    new_kv,
    prompt_kv,
    suffix_kv,
    lengths,
    w_out,
    moe_gain,
    w_router,
    expert_weights,
    old_lines,
    new_lines,
    routes,
):
    experts, line_count, parts, width = expert_weights.shape
    seqs = hidden.shape[0]
    tokens = seqs * row_count
    share = tokens // col_count
    per_peer = experts * line_count // row_count
    block = rounded_up(per_peer, 16)
    row_far, row_near = split(row_count)
    col_far, col_near = split(col_count)
    vmem = pl.BlockSpec(memory_space=pltpu.VMEM)
    rows = 2 * seqs
    layer_out, moved = pl.pallas_call(
        functools.partial(step_kernel, row_count, col_count),
        out_shape=(
            jax.ShapeDtypeStruct((seqs, width), f32),
            jax.ShapeDtypeStruct((experts, parts, line_count, width), bf16),
        ),
        in_specs=[pl.BlockSpec(memory_space=pltpu.SMEM)] + [vmem] * 12,
        out_specs=(vmem, vmem),
        scratch_shapes=[
            pltpu.VMEM((col_near, col_far, 2 * rows, HD), bf16),
            pltpu.VMEM((col_near, col_far, 2 * rows, HD), bf16),
            pltpu.VMEM((col_far, 2 * rows, HD), bf16),
            pltpu.VMEM((col_far, 2 * rows, HD), bf16),
            pltpu.VMEM((col_near, col_far, rows, HD), bf16),
            pltpu.VMEM((row_near, row_far, rows, width), bf16),
            pltpu.VMEM((384, experts * width), bf16),
            pltpu.VMEM((col_near, col_far, 2, share, 384), bf16),
            pltpu.VMEM((col_near, col_far, 2, share, 384), bf16),
            pltpu.VMEM((col_far, 2, share, 384), bf16),
            pltpu.VMEM((col_far, 2, share, 384), bf16),
            pltpu.VMEM((col_near, col_far, 3, share, 128), bf16),
            pltpu.VMEM((experts, 256, width), bf16),
            pltpu.VMEM((row_near, row_far, seqs, width), bf16),
            pltpu.VMEM((row_near, row_far, seqs, width), bf16),
            pltpu.VMEM((row_far, seqs, width), bf16),
            pltpu.VMEM((row_far, seqs, width), bf16),
            pltpu.VMEM((row_count, block, parts * width), bf16),
            pltpu.VMEM((row_count, block, parts * width), bf16),
            pltpu.VMEM((experts, line_count, 128), f32),
            pltpu.SemaphoreType.DMA((13,)),
            pltpu.SemaphoreType.DMA((13,)),
        ],
        compiler_params=pltpu.CompilerParams(
            collective_id=0, has_side_effects=True, vmem_limit_bytes=56 << 20
        ),
        name="decode_step",
    )(
        lengths,
        hidden,
        queries,
        new_kv,
        prompt_kv,
        suffix_kv,
        w_out,
        moe_gain.reshape(1, width),
        jnp.transpose(w_router),
        jnp.transpose(expert_weights, (0, 2, 1, 3)),
        old_lines,
        new_lines,
        jnp.transpose(routes),
    )
    return layer_out, jnp.transpose(moved, (0, 2, 1, 3))


def solution(mesh):
    return jax.shard_map(
        functools.partial(local, mesh.shape["row"], mesh.shape["col"]),
        mesh=mesh,
        in_specs=(
            P("row", "col"),
            P("row", None),
            P("row", None, None),
            P("row", None, "col", None),
            P("row", None, "col", None),
            P("row"),
            P(None, "col"),
            P("col"),
            P("col", None),
            P(None, "row", None, "col"),
            P(),
            P(),
            P(),
        ),
        out_specs=(P("row", "col"), P(None, "row", None, "col")),
        check_vma=False,
    )
```

time: 146 us -> 110 us (0.75)
  Pallas kernels: 126 us -> 105 us
  other arithmetic: 12.8 us -> 0 us
  local copies, waits for them, and re-layouts: 6.36 us -> 3.56 us
    pallas_call x1, Pallas kernels: 126 us -> 105 us  [local(): pl.pallas_call(functools.partial(step_kernel, row_count, col_count), out_...]
    reduce_sum x3 -> x0, other arithmetic: 10.9 us -> none  [the longest x1 9.06 us: owner_slots(): jnp.sum(jnp.where(ids[:, :, None] == table[:, None, :], owners[None, None...]
    add x3 -> x0, other arithmetic: 1.85 us -> none  [the longest x1 1.17 us: local(): take_slots = place + (distance - source) * block]
    unnamed x3 -> x2, local copies, waits for them, and re-layouts: 5.03 us -> 3.56 us
where the time goes in v2:
time: 110 us; the launch traced here: 109 us
  Pallas kernels  105 us (95%)
  local copies, waits for them, and re-layouts  3.56 us (3%)
    pallas_call x1, Pallas kernels, local(): pl.pallas_call(functools.partial(step_kernel, row_count, col_count), out_...  105 us
    unnamed x2, local copies, waits for them, and re-layouts  3.56 us

profile of v2, /device:TPU:1, one launch (start us, length us, event | category | flops | bytes accessed | tf_op | source)
XLA Modules:
  0.0 108.8 jit_solution(14327977301193467037)
XLA Ops:
  0.6 104.6 %decode_step.1 = (f32[8,128]{1,0:T(8,128)}, bf16[8,3,176,128]{3,2,1,0:T(8,128)(2,1)}) custom-call(s32[8]{0:T(128)} %lengths_ref.1, bf16[8,128]{1,0:T(8,128)(2,1)} %hidden_ref.1, bf16[8,4096]{1,0:T(8,128)(2,1)} %queries_ref.1, bf16[8,2,2048]{2,1,0:T(2,128)(2,1)} %new_kv_ref.1, bf16[1,2,64,2048]{3,2,1,0:T(8,128)(2,1)} %prompt_ref.1, ...), custom_call_target="tpu_custom_call" | custom-call | tf_op jit(solution)/shard_map/decode_step/pallas_call | solution.py:587
  105.3 1.3 %copy.17 = f32[8,128]{1,0:T(8,128)} copy(f32[8,128]{1,0:T(8,128)} %get-tuple-element.8) | data formatting | bytes 8192
  106.5 2.3 %copy.18 = bf16[8,176,3,128]{3,1,2,0:T(8,128)(2,1)} copy(bf16[8,176,3,128]{3,1,2,0:T(8,128)(2,1)} %bitcast.6) | data formatting | bytes 2162688

commit v3 on v2

--- a/solution.py
+++ b/solution.py
@@ -12,8 +12,9 @@
 neg_big = -1e30
 f32 = jnp.float32
 bf16 = jnp.bfloat16
+i16 = jnp.int16
 MESH = pl.DeviceIdType.MESH
-MOVES = (0, 3, 6, 9, 12, 15, 18, 21, 24, 27, 29, 31)
+MOVES = (0, 2, 5, 7, 10, 12, 15, 17, 20, 23, 27, 31)
 
 
 def rounded_up(value, step):
@@ -48,36 +49,63 @@
         far = lax.rem(row // near_count - owner_lane // near_count + 128 * far_count, far_count)
         near = lax.rem(row % near_count - owner_lane % near_count + near_count, near_count)
         offsets = (near * far_count + far).astype(f32) * block
-    counts = jnp.zeros((1, 128), f32)
+    tiles = line_count // 16
+    wanted = [
+        jnp.broadcast_to(id_columns[:, e : e + 1], (line_count, 128))
+        .astype(jnp.int32)
+        .astype(i16)
+        .reshape(tiles, 16, 128)
+        for e in range(experts)
+    ]
+
+    def rows16(row):
+        return jnp.broadcast_to(row, (16, 128)).astype(i16)[None]
+
+    found = []
+    for e in range(0, experts, 2):
+
+        def search(chunk, both):
+            at = chunk * 128
+            first = at // line_count
+            owner = rows16(first + jnp.where(owner_lane + at >= (first + 1) * line_count, 1, 0))
+            return tuple(
+                jnp.where(
+                    wanted[e + i]
+                    == rows16(
+                        table_ref[e + i : e + i + 1, pl.ds(pl.multiple_of(at, 128), 128)]
+                    ),
+                    owner,
+                    both[i],
+                )
+                for i in range(2)
+            )
+
+        none = jnp.zeros((tiles, 16, 128), i16)
+        found += lax.fori_loop(0, full // 128, search, (none, none), unroll=4)
+    owner_columns = [
+        jnp.sum(
+            one.reshape(line_count, 128).astype(jnp.int32).astype(f32), axis=1, keepdims=True
+        )
+        for one in found
+    ]
+    hits = [jnp.where(column == owners_f32, 1.0, 0.0) for column in owner_columns]
+    counts = [jnp.zeros((1, 128), f32)]
+    for e in range(experts - 1):
+        counts.append(counts[e] + jnp.sum(hits[e], axis=0, keepdims=True))
+    fill = jnp.zeros((5, 128), f32)
     slots = []
     for e in range(experts):
+        pack = jnp.concatenate([counts[e], offsets, owners_f32, fill], axis=0)
+        looked = dot_nt(pack.astype(bf16), hits[e].astype(bf16))
+        id_row = id_rows[e : e + 1, 0:line_count]
         id_column = id_columns[:, e : e + 1]
-        wanted = jnp.broadcast_to(id_column, (line_count, 128)).astype(jnp.int32)
-
-        def search(chunk, found):
-            at = chunk * 128
-            table = table_ref[e : e + 1, pl.ds(pl.multiple_of(at, 128), 128)]
-            first = at // line_count
-            owner = first + jnp.where(owner_lane + at >= (first + 1) * line_count, 1, 0)
-            return jnp.where(wanted == table, owner, found)
-
-        found = lax.fori_loop(
-            0, full // 128, search, jnp.zeros((line_count, 128), jnp.int32), unroll=4
-        )
-        owner_column = jnp.sum(found.astype(f32), axis=1, keepdims=True)
-        hits = jnp.where(owner_column == owners_f32, 1.0, 0.0)
-        pack = jnp.concatenate([counts, offsets, owners_f32, jnp.zeros((5, 128), f32)], axis=0)
-        looked = dot_nt(pack.astype(bf16), hits.astype(bf16))
-        owner_row = looked[2:3]
-        id_row = id_rows[e : e + 1, 0:line_count]
-        same = owner_column == owner_row
+        same = owner_columns[e] == looked[2:3]
         if outgoing:
             rank = jnp.sum(jnp.where(same & (id_column < id_row), 1.0, 0.0), axis=0, keepdims=True)
             slots.append(rank + looked[0:1] + looked[1:2])
         else:
             rank = jnp.sum(jnp.where(same & (id_row < id_column), 1.0, 0.0), axis=1, keepdims=True)
-            slots.append(rank + jnp.sum(hits * (counts + offsets), axis=1, keepdims=True))
-        counts = counts + jnp.sum(hits, axis=0, keepdims=True)
+            slots.append(rank + jnp.sum(hits[e] * (counts[e] + offsets), axis=1, keepdims=True))
     return slots
 
 
@@ -90,10 +118,10 @@
     new_kv_ref,
     prompt_ref,
     suffix_ref,
-    w_out_ref,
+    w_out_hbm,
     gain_ref,
     router_ref,
-    lines_ref,
+    lines_hbm,
     old_lines_ref,
     new_lines_ref,
     routes_ref,
@@ -119,18 +147,27 @@
     move_out,
     move_in,
     take_slots,
+    flat_lines,
+    w_out_ref,
+    lines_ref,
+    local_sems,
     send_sems,
     recv_sems,
 ):
     row = lax.axis_index("row")
     col = lax.axis_index("col")
     seqs = hidden_ref.shape[0]
-    experts, _, line_count, width = lines_ref.shape
+    experts, _, line_count, width = lines_hbm.shape
     prompt_rows = prompt_ref.shape[2]
     suffix_rows = suffix_ref.shape[2]
     tokens = seqs * row_count
     share = tokens // col_count
     score_scale = HD ** (-0.5)
+
+    w_out_copy = pltpu.make_async_copy(w_out_hbm, w_out_ref, local_sems.at[0])
+    lines_copy = pltpu.make_async_copy(lines_hbm, lines_ref, local_sems.at[1])
+    lines_copy.start()
+    w_out_copy.start()
 
     barrier = pltpu.get_barrier_semaphore()
     row_far_count, row_near_count = split(row_count)
@@ -241,31 +278,51 @@
     per_peer = experts * line_count // row_count
     block = move_out.shape[1]
     slots = line_slots(row, row_count, block, old_lines_ref, new_lines_ref, line_count, True)
-    peers_at_once = 4
+    padded = 256
+    spare_lanes = jnp.full((1, padded - line_count), -1.0, f32)
+    send_slots = jnp.concatenate(
+        [part for e in range(experts) for part in (slots[e], spare_lanes)], axis=1
+    ).astype(jnp.int32)
+    send_slots = jnp.broadcast_to(send_slots, (16, experts * padded)).astype(i16)[None]
+    peers_at_once = row_count // 2
     chunk = peers_at_once * block
-
-    def sort_chunk(at, carry):
-        wanted = (
-            at * chunk + lax.broadcasted_iota(jnp.int32, (chunk, line_count), 0)
-        ).astype(f32)
-        sorted_lines = jnp.zeros((chunk, 3 * width), f32)
-        for e in range(experts):
-            picks = jnp.where(wanted == slots[e], 1.0, 0.0).astype(bf16)
-            lines = jnp.concatenate([lines_ref[e, j] for j in range(3)], axis=1)
-            sorted_lines = sorted_lines + jnp.dot(picks, lines, preferred_element_type=f32)
-        move_out[pl.ds(at * peers_at_once, peers_at_once)] = (
-            sorted_lines.astype(bf16).reshape(peers_at_once, block, 3 * width)
+    lines_copy.wait()
+    for e in range(experts):
+        at = e * padded
+        for j in range(3):
+            flat_lines[at : at + line_count, j * width : (j + 1) * width] = lines_ref[e, j]
+        flat_lines[at + line_count : at + padded, :] = jnp.zeros(
+            (padded - line_count, 3 * width), bf16
         )
-        return carry
+    one, zero = jnp.ones((), bf16), jnp.zeros((), bf16)
+
+    def sort_lines(at):
+        shape = (chunk // 16, 16, experts * padded)
+        place = (
+            lax.broadcasted_iota(jnp.int32, (chunk, 128), 0) + at * chunk
+        ).astype(i16).reshape(chunk // 16, 16, 128)
+        picks = jnp.concatenate(
+            [
+                jnp.where(place == send_slots[:, :, k * 128 : (k + 1) * 128], one, zero)
+                for k in range(experts * padded // 128)
+            ],
+            axis=2,
+        ).reshape(chunk, experts * padded)
+        sorted_lines = jnp.dot(picks, flat_lines[...], preferred_element_type=f32).astype(bf16)
+        move_out[pl.ds(at * peers_at_once, peers_at_once)] = sorted_lines.reshape(
+            peers_at_once, block, 3 * width
+        )
 
     moves = [1 + (row_count - 1) * share_of // 31 for share_of in MOVES]
+
+    early = row_count // 2
 
     def move(batch):
         send(
             row_peer,
             moves[batch],
             moves[batch + 1],
-            12,
+            12 if moves[batch + 1] <= early else 13,
             lambda peer: move_out.at[peer],
             lambda k: move_in.at[k],
         )
@@ -302,7 +359,8 @@
         lambda peer: joined_out.at[peer],
         lambda k: joined_in.at[k],
     )
-    lax.fori_loop(0, row_count // peers_at_once, sort_chunk, 0)
+    sort_lines(0)
+    sort_lines(1)
     move_in[0] = move_out[row]
     move(0)
 
@@ -352,6 +410,7 @@
     )
     move(2)
     wait(3, near_heads, recv_sems)
+    w_out_copy.wait()
     projected = jnp.zeros((rows, 2 * width), f32)
     for k in range(col_near_count):
         near = lax.rem(col_near + col_near_count - k, col_near_count)
@@ -379,7 +438,7 @@
     for e, slots in enumerate(
         line_slots(row, row_count, block, new_lines_ref, old_lines_ref, line_count, False)
     ):
-        take_slots[e] = jnp.broadcast_to(slots, (line_count, 128))
+        take_slots[e] = jnp.broadcast_to(slots, (line_count, 128)).astype(jnp.int32).astype(i16)
     routes = [
         jnp.transpose(jnp.broadcast_to(routes_ref[k : k + 1, :].astype(f32), (width, tokens)))
         for k in range(2)
@@ -533,26 +592,40 @@
     )
     move(10)
     nearer_in[0] = nearer_out[row_far]
+
+    early_moved = move_in.at[pl.ds(1, early - 1)]
+    late_moved = move_in.at[pl.ds(early, row_count - early)]
+
+    def place_lines(start, add):
+        here = move_in[pl.ds(start, early)].reshape(early * block, 3 * width)
+        place = lax.broadcasted_iota(jnp.int32, (16, 128), 1) + start * block
+        at_once = experts // 2
+        for e in range(0, experts, at_once):
+            taken = take_slots[e : e + at_once].reshape(at_once * line_count // 16, 16, 128)
+            picks = jnp.concatenate(
+                [
+                    jnp.where(taken == (place + k * 128).astype(i16)[None], one, zero)
+                    for k in range(early * block // 128)
+                ],
+                axis=2,
+            ).reshape(at_once * line_count, early * block)
+            placed = jnp.dot(picks, here, preferred_element_type=f32).astype(bf16)
+            for i in range(at_once):
+                for j in range(3):
+                    part = placed[i * line_count : (i + 1) * line_count, j * width : (j + 1) * width]
+                    moved_ref[e + i, j] = moved_ref[e + i, j] + part if add else part
+
+    wait(12, early_moved, recv_sems)
+    place_lines(0, False)
     wait(11, far_mixed, recv_sems)
     layer_ref[...] = h_float + jnp.sum(nearer_in[...].astype(f32), axis=0)
 
-    moved = move_in.at[pl.ds(1, row_count - 1)]
-    wait(12, moved, recv_sems)
-    everything = move_in[...].reshape(row_count * block, 3 * width)
-
-    def place(e, carry):
-        slots = take_slots[e][:, 0:1]
-        held = lax.broadcasted_iota(jnp.int32, (line_count, row_count * block), 1).astype(f32)
-        picks = jnp.where(held == slots, 1.0, 0.0).astype(bf16)
-        placed = jnp.dot(picks, everything, preferred_element_type=f32).astype(bf16)
-        for j in range(3):
-            moved_ref[e, j] = placed[:, j * width : (j + 1) * width]
-        return carry
-
-    lax.fori_loop(0, experts, place, 0)
+    wait(13, late_moved, recv_sems)
+    place_lines(early, True)
 
     sent = [near_parts, far_parts, far_heads, near_heads, far_tokens, near_tokens, near_sums]
-    sent += [far_sums, far_acts, near_acts, near_mixed, far_mixed, moved]
+    sent += [far_sums, far_acts, near_acts, near_mixed, far_mixed, early_moved]
+    sent += [late_moved]
     for lane, copies in enumerate(sent):
         wait(lane, copies, send_sems)
 
@@ -583,6 +656,7 @@
     row_far, row_near = split(row_count)
     col_far, col_near = split(col_count)
     vmem = pl.BlockSpec(memory_space=pltpu.VMEM)
+    hbm = pl.BlockSpec(memory_space=pl.ANY)
     rows = 2 * seqs
     layer_out, moved = pl.pallas_call(
         functools.partial(step_kernel, row_count, col_count),
@@ -590,7 +664,7 @@
             jax.ShapeDtypeStruct((seqs, width), f32),
             jax.ShapeDtypeStruct((experts, parts, line_count, width), bf16),
         ),
-        in_specs=[pl.BlockSpec(memory_space=pltpu.SMEM)] + [vmem] * 12,
+        in_specs=[pl.BlockSpec(memory_space=pltpu.SMEM)] + [vmem] * 5 + [hbm, vmem, vmem, hbm] + [vmem] * 3,
         out_specs=(vmem, vmem),
         scratch_shapes=[
             pltpu.VMEM((col_near, col_far, 2 * rows, HD), bf16),
@@ -612,9 +686,13 @@
             pltpu.VMEM((row_far, seqs, width), bf16),
             pltpu.VMEM((row_count, block, parts * width), bf16),
             pltpu.VMEM((row_count, block, parts * width), bf16),
-            pltpu.VMEM((experts, line_count, 128), f32),
-            pltpu.SemaphoreType.DMA((13,)),
-            pltpu.SemaphoreType.DMA((13,)),
+            pltpu.VMEM((experts, line_count, 128), i16),
+            pltpu.VMEM((experts * 256, parts * width), bf16),
+            pltpu.VMEM(w_out.shape, bf16),
+            pltpu.VMEM((experts, parts, line_count, width), bf16),
+            pltpu.SemaphoreType.DMA((2,)),
+            pltpu.SemaphoreType.DMA((14,)),
+            pltpu.SemaphoreType.DMA((14,)),
         ],
         compiler_params=pltpu.CompilerParams(
             collective_id=0, has_side_effects=True, vmem_limit_bytes=56 << 20

time: 110 us -> 104 us (0.945)
  the two profiles are of different devices: /device:TPU:1 before, /device:TPU:33 now
where the time goes in v3:
time: 104 us; the launch traced here: 103 us
  Pallas kernels  99.2 us (95%)
  local copies, waits for them, and re-layouts  3.56 us (3%)
    pallas_call x1, Pallas kernels, local(): pl.pallas_call(functools.partial(step_kernel, row_count, col_count), out_...  99.2 us
    unnamed x2, local copies, waits for them, and re-layouts  3.56 us

profile of v3, /device:TPU:33, one launch (start us, length us, event | category | flops | bytes accessed | tf_op | source)
XLA Modules:
  0.0 103.4 jit_solution(7786280647479625457)
XLA Ops:
  0.6 99.2 %decode_step.1 = (f32[8,128]{1,0:T(8,128)}, bf16[8,3,176,128]{3,2,1,0:T(8,128)(2,1)}) custom-call(s32[8]{0:T(128)} %lengths_ref.1, bf16[8,128]{1,0:T(8,128)(2,1)} %hidden_ref.1, bf16[8,4096]{1,0:T(8,128)(2,1)} %queries_ref.1, bf16[8,2,2048]{2,1,0:T(2,128)(2,1)} %new_kv_ref.1, bf16[1,2,64,2048]{3,2,1,0:T(8,128)(2,1)} %prompt_ref.1, ...), custom_call_target="tpu_custom_call" | custom-call | tf_op jit(solution)/shard_map/decode_step/pallas_call | solution.py:661
  99.8 1.3 %copy.17 = f32[8,128]{1,0:T(8,128)} copy(f32[8,128]{1,0:T(8,128)} %get-tuple-element.8) | data formatting | bytes 8192
  101.1 2.3 %copy.18 = bf16[8,176,3,128]{3,1,2,0:T(8,128)(2,1)} copy(bf16[8,176,3,128]{3,1,2,0:T(8,128)(2,1)} %bitcast.6) | data formatting | bytes 2162688

commit v4 on v3

--- a/solution.py
+++ b/solution.py
@@ -14,7 +14,7 @@
 bf16 = jnp.bfloat16
 i16 = jnp.int16
 MESH = pl.DeviceIdType.MESH
-MOVES = (0, 2, 5, 7, 10, 12, 15, 17, 20, 23, 27, 31)
+MOVES = (0, 3, 6, 9, 12, 15, 18, 21, 24, 28, 31)
 
 
 def rounded_up(value, step):
@@ -317,14 +317,22 @@
 
     early = row_count // 2
 
+    def mirrored(k):
+        far = k % row_far_count
+        turned = lax.rem(row_far_count - far, row_far_count)
+        return k - far + jnp.where(row_near % 2 == 1, turned, far)
+
+    def move_peer(k):
+        return row_peer(mirrored(k))
+
     def move(batch):
         send(
-            row_peer,
+            move_peer,
             moves[batch],
             moves[batch + 1],
-            12 if moves[batch + 1] <= early else 13,
+            11 if moves[batch + 1] <= early else 12,
             lambda peer: move_out.at[peer],
-            lambda k: move_in.at[k],
+            lambda k: move_in.at[mirrored(k)],
         )
 
     def join(parts, tops):
@@ -356,7 +364,7 @@
         1,
         col_far_count,
         1,
-        lambda peer: joined_out.at[peer],
+        lambda peer: joined_out,
         lambda k: joined_in.at[k],
     )
     sort_lines(0)
@@ -364,22 +372,33 @@
     move_in[0] = move_out[row]
     move(0)
 
-    joined_in[0] = joined_out[col_far]
-    own_query = query_rows(pl.multiple_of(col * 2 * HD, 2 * HD))
-    own_pair = new_kv_ref[:, :, pl.ds(pl.multiple_of(col * HD, HD), HD)].astype(f32)
-    own_key = jnp.concatenate([own_pair[:, 0, :]] * 2, axis=0)
-    own_value = jnp.concatenate([own_pair[:, 1, :]] * 2, axis=0)
-    own_score = jnp.sum(own_query * own_key, axis=1, keepdims=True) * score_scale
+    joined_in[0] = joined_out[...]
+    own_pairs = []
+    for far in range(col_far_count):
+        head = far * col_near_count + col_near
+        own_query = query_rows(pl.multiple_of(head * 2 * HD, 2 * HD))
+        own_pair = new_kv_ref[:, :, pl.ds(pl.multiple_of(head * HD, HD), HD)].astype(f32)
+        own_key = jnp.concatenate([own_pair[:, 0, :]] * 2, axis=0)
+        own_value = jnp.concatenate([own_pair[:, 1, :]] * 2, axis=0)
+        own_score = jnp.sum(own_query * own_key, axis=1, keepdims=True) * score_scale
+        own_pairs.append((own_score, own_value))
     wait(1, far_parts, recv_sems)
-    parts = [joined_in[k] for k in range(col_far_count)]
-    top, total, mixture = join(parts, [top_of(part) for part in parts] + [own_score])
-    own_weight = jnp.exp(own_score - top)
-    mixture = mixture + own_weight.astype(bf16).astype(f32) * own_value
-    heads_in[0, col_far] = (mixture / (total + own_weight)).astype(bf16)
-    own_heads = heads_in.at[0, col_far]
-    far_heads = heads_in.at[0, pl.ds(0, col_far_count - 1)]
+    for far in range(col_far_count):
+        own_score, own_value = own_pairs[far]
+        parts = [joined_in[k, far] for k in range(col_far_count)]
+        top, total, mixture = join(parts, [top_of(part) for part in parts] + [own_score])
+        own_weight = jnp.exp(own_score - top)
+        mixture = mixture + own_weight.astype(bf16).astype(f32) * own_value
+        heads_in[0, far] = (mixture / (total + own_weight)).astype(bf16)
     near_heads = heads_in.at[pl.ds(1, col_near_count - 1)]
-    send(col_far_peer, 1, col_far_count, 2, lambda peer: own_heads, lambda k: own_heads)
+    send(
+        col_near_peer,
+        1,
+        col_near_count,
+        2,
+        lambda peer: heads_in.at[0],
+        lambda k: heads_in.at[k],
+    )
     move(1)
 
     tail = line_count - 128
@@ -399,17 +418,7 @@
         down[e, 192 : 192 + tail, :] = lines_ref[e, 2, 128:line_count, :]
         down[e, 192 + tail : 256, :] = gap
 
-    wait(2, far_heads, recv_sems)
-    send(
-        col_near_peer,
-        1,
-        col_near_count,
-        3,
-        lambda peer: heads_in.at[0],
-        lambda k: heads_in.at[k],
-    )
-    move(2)
-    wait(3, near_heads, recv_sems)
+    wait(2, near_heads, recv_sems)
     w_out_copy.wait()
     projected = jnp.zeros((rows, 2 * width), f32)
     for k in range(col_near_count):
@@ -432,8 +441,8 @@
     own_tokens = token_in.at[row_near, row_far]
     far_tokens = token_in.at[0, pl.ds(0, row_far_count - 1)]
     near_tokens = token_in.at[pl.ds(0, row_near_count - 1)]
-    send(row_far_peer, 1, row_far_count, 4, lambda peer: own_tokens, lambda k: own_tokens)
-    move(3)
+    send(row_far_peer, 1, row_far_count, 3, lambda peer: own_tokens, lambda k: own_tokens)
+    move(2)
 
     for e, slots in enumerate(
         line_slots(row, row_count, block, new_lines_ref, old_lines_ref, line_count, False)
@@ -444,11 +453,11 @@
         for k in range(2)
     ]
 
-    wait(4, far_tokens, recv_sems)
+    wait(3, far_tokens, recv_sems)
     own_tokens = token_in.at[row_near]
-    send(row_near_peer, 1, row_near_count, 5, lambda peer: own_tokens, lambda k: own_tokens)
-    move(4)
-    wait(5, near_tokens, recv_sems)
+    send(row_near_peer, 1, row_near_count, 4, lambda peer: own_tokens, lambda k: own_tokens)
+    move(3)
+    wait(4, near_tokens, recv_sems)
     everything = token_in[...].astype(f32)
     by_row = [everything[r % row_near_count, r // row_near_count] for r in range(row_count)]
     every_token = jnp.concatenate([part[0:seqs] for part in by_row], axis=0)
@@ -485,14 +494,14 @@
         col_near_peer,
         1,
         col_near_count,
-        6,
+        5,
         lambda peer: summed_out.at[peer],
         lambda k: summed_in.at[k],
     )
-    move(5)
+    move(4)
 
     summed_in[0] = summed_out[col_near]
-    wait(6, near_sums, recv_sems)
+    wait(5, near_sums, recv_sems)
     for far in range(col_far_count):
         sums = summed_in[0, far].astype(f32)
         for k in range(1, col_near_count):
@@ -506,13 +515,13 @@
         col_far_peer,
         1,
         col_far_count,
-        7,
+        6,
         lambda peer: halved_out.at[peer],
         lambda k: halved_in.at[k],
     )
-    move(6)
+    move(5)
     halved_in[0] = halved_out[col_far]
-    wait(7, far_sums, recv_sems)
+    wait(6, far_sums, recv_sems)
     sums = halved_in[0].astype(f32)
     for k in range(1, col_far_count):
         sums = sums + halved_in[k].astype(f32)
@@ -544,14 +553,14 @@
     own_acts = act_in.at[col_near, col_far]
     far_acts = act_in.at[0, pl.ds(0, col_far_count - 1)]
     near_acts = act_in.at[pl.ds(0, col_near_count - 1)]
-    send(col_far_peer, 1, col_far_count, 8, lambda peer: own_acts, lambda k: own_acts)
+    send(col_far_peer, 1, col_far_count, 7, lambda peer: own_acts, lambda k: own_acts)
+    move(6)
+    wait(7, far_acts, recv_sems)
+    own_row = act_in.at[col_near]
+    send(col_near_peer, 1, col_near_count, 8, lambda peer: own_row, lambda k: own_row)
     move(7)
-    wait(8, far_acts, recv_sems)
-    own_row = act_in.at[col_near]
-    send(col_near_peer, 1, col_near_count, 9, lambda peer: own_row, lambda k: own_row)
-    move(8)
-
-    wait(9, near_acts, recv_sems)
+
+    wait(8, near_acts, recv_sems)
     by_col = [act_in[c % col_near_count, c // col_near_count] for c in range(col_count)]
     firsts = [
         jnp.concatenate([part[k] for part in by_col], axis=0).astype(f32) for k in range(2)
@@ -574,23 +583,23 @@
         row_near_peer,
         1,
         row_near_count,
-        10,
+        9,
         lambda peer: mixed_out.at[peer],
         lambda k: mixed_in.at[k],
     )
-    move(9)
+    move(8)
     mixed_in[0] = mixed_out[row_near]
-    wait(10, near_mixed, recv_sems)
+    wait(9, near_mixed, recv_sems)
     nearer_out[...] = jnp.sum(mixed_in[...].astype(f32), axis=0).astype(bf16)
     send(
         row_far_peer,
         1,
         row_far_count,
-        11,
+        10,
         lambda peer: nearer_out.at[peer],
         lambda k: nearer_in.at[k],
     )
-    move(10)
+    move(9)
     nearer_in[0] = nearer_out[row_far]
 
     early_moved = move_in.at[pl.ds(1, early - 1)]
@@ -615,15 +624,15 @@
                     part = placed[i * line_count : (i + 1) * line_count, j * width : (j + 1) * width]
                     moved_ref[e + i, j] = moved_ref[e + i, j] + part if add else part
 
-    wait(12, early_moved, recv_sems)
+    wait(11, early_moved, recv_sems)
     place_lines(0, False)
-    wait(11, far_mixed, recv_sems)
+    wait(10, far_mixed, recv_sems)
     layer_ref[...] = h_float + jnp.sum(nearer_in[...].astype(f32), axis=0)
 
-    wait(13, late_moved, recv_sems)
+    wait(12, late_moved, recv_sems)
     place_lines(early, True)
 
-    sent = [near_parts, far_parts, far_heads, near_heads, far_tokens, near_tokens, near_sums]
+    sent = [near_parts, far_parts, near_heads, far_tokens, near_tokens, near_sums]
     sent += [far_sums, far_acts, near_acts, near_mixed, far_mixed, early_moved]
     sent += [late_moved]
     for lane, copies in enumerate(sent):
@@ -670,7 +679,7 @@
             pltpu.VMEM((col_near, col_far, 2 * rows, HD), bf16),
             pltpu.VMEM((col_near, col_far, 2 * rows, HD), bf16),
             pltpu.VMEM((col_far, 2 * rows, HD), bf16),
-            pltpu.VMEM((col_far, 2 * rows, HD), bf16),
+            pltpu.VMEM((col_far, col_far, 2 * rows, HD), bf16),
             pltpu.VMEM((col_near, col_far, rows, HD), bf16),
             pltpu.VMEM((row_near, row_far, rows, width), bf16),
             pltpu.VMEM((384, experts * width), bf16),
@@ -691,8 +700,8 @@
             pltpu.VMEM(w_out.shape, bf16),
             pltpu.VMEM((experts, parts, line_count, width), bf16),
             pltpu.SemaphoreType.DMA((2,)),
-            pltpu.SemaphoreType.DMA((14,)),
-            pltpu.SemaphoreType.DMA((14,)),
+            pltpu.SemaphoreType.DMA((13,)),
+            pltpu.SemaphoreType.DMA((13,)),
         ],
         compiler_params=pltpu.CompilerParams(
             collective_id=0, has_side_effects=True, vmem_limit_bytes=56 << 20

time: 104 us -> 100 us (0.962)
  the two profiles are of different devices: /device:TPU:33 before, /device:TPU:1 now
where the time goes in v4:
time: 100 us
  Pallas kernels  95.9 us (96%)
  local copies, waits for them, and re-layouts  3.56 us (4%)
    pallas_call x1, Pallas kernels, local(): pl.pallas_call(functools.partial(step_kernel, row_count, col_count), out_...  95.9 us
    unnamed x2, local copies, waits for them, and re-layouts  3.56 us

profile of v4, /device:TPU:1, one launch (start us, length us, event | category | flops | bytes accessed | tf_op | source)
XLA Modules:
  0.0 100.1 jit_solution(11481924259340926194)
XLA Ops:
  0.6 95.9 %decode_step.1 = (f32[8,128]{1,0:T(8,128)}, bf16[8,3,176,128]{3,2,1,0:T(8,128)(2,1)}) custom-call(s32[8]{0:T(128)} %lengths_ref.1, bf16[8,128]{1,0:T(8,128)(2,1)} %hidden_ref.1, bf16[8,4096]{1,0:T(8,128)(2,1)} %queries_ref.1, bf16[8,2,2048]{2,1,0:T(2,128)(2,1)} %new_kv_ref.1, bf16[1,2,64,2048]{3,2,1,0:T(8,128)(2,1)} %prompt_ref.1, ...), custom_call_target="tpu_custom_call" | custom-call | tf_op jit(solution)/shard_map/decode_step/pallas_call | solution.py:670
  96.6 1.3 %copy.17 = f32[8,128]{1,0:T(8,128)} copy(f32[8,128]{1,0:T(8,128)} %get-tuple-element.8) | data formatting | bytes 8192
  97.9 2.3 %copy.18 = bf16[8,176,3,128]{3,1,2,0:T(8,128)(2,1)} copy(bf16[8,176,3,128]{3,1,2,0:T(8,128)(2,1)} %bitcast.6) | data formatting | bytes 2162688

commit v5 on v4

--- a/solution.py
+++ b/solution.py
@@ -14,7 +14,7 @@
 bf16 = jnp.bfloat16
 i16 = jnp.int16
 MESH = pl.DeviceIdType.MESH
-MOVES = (0, 3, 6, 9, 12, 15, 18, 21, 24, 28, 31)
+MOVES = (0, 4, 6, 10, 12, 15, 19, 22, 25, 27, 31)
 
 
 def rounded_up(value, step):

time: 100 us -> 99.6 us (level); the launches traced: 100 us -> 98.6 us
  Pallas kernels: 95.9 us -> 94.4 us
    pallas_call x1, Pallas kernels: 95.9 us -> 94.4 us  [local(): pl.pallas_call(functools.partial(step_kernel, row_count, col_count), out_...]
where the time goes in v5:
time: 99.6 us; the launch traced here: 98.6 us
  Pallas kernels  94.4 us (95%)
  local copies, waits for them, and re-layouts  3.56 us (4%)
    pallas_call x1, Pallas kernels, local(): pl.pallas_call(functools.partial(step_kernel, row_count, col_count), out_...  94.4 us
    unnamed x2, local copies, waits for them, and re-layouts  3.56 us

profile of v5, /device:TPU:1, one launch (start us, length us, event | category | flops | bytes accessed | tf_op | source)
XLA Modules:
  0.0 98.6 jit_solution(2486013048928548405)
XLA Ops:
  0.6 94.4 %decode_step.1 = (f32[8,128]{1,0:T(8,128)}, bf16[8,3,176,128]{3,2,1,0:T(8,128)(2,1)}) custom-call(s32[8]{0:T(128)} %lengths_ref.1, bf16[8,128]{1,0:T(8,128)(2,1)} %hidden_ref.1, bf16[8,4096]{1,0:T(8,128)(2,1)} %queries_ref.1, bf16[8,2,2048]{2,1,0:T(2,128)(2,1)} %new_kv_ref.1, bf16[1,2,64,2048]{3,2,1,0:T(8,128)(2,1)} %prompt_ref.1, ...), custom_call_target="tpu_custom_call" | custom-call | tf_op jit(solution)/shard_map/decode_step/pallas_call | solution.py:670
  95.1 1.3 %copy.17 = f32[8,128]{1,0:T(8,128)} copy(f32[8,128]{1,0:T(8,128)} %get-tuple-element.8) | data formatting | bytes 8192
  96.4 2.3 %copy.18 = bf16[8,176,3,128]{3,1,2,0:T(8,128)(2,1)} copy(bf16[8,176,3,128]{3,1,2,0:T(8,128)(2,1)} %bitcast.6) | data formatting | bytes 2162688
